TPU v7x, 512 devices: a whole 4x4x16 slice. The times are simulated.
512 devices in a mesh: tmpl: 2 (over x_lo), row: 16 (over y, x_hi, core), col: 16 (over z).
Axes of the slice: x: 4 (x_hi: 2, x_lo: 2; x = x_hi * 2 + x_lo), y: 4, z: 16, core: 2. Of those that a mesh axis runs over, the one named last changes fastest.
Arguments:
- pair: bfloat16 [2, 512, 32768], P('tmpl', 'row', 'col'), may hold values from -6 to 6
- saved_product: bfloat16 [2, 512, 32768], P('tmpl', 'row', 'col'), may hold values from -32 to 32
- out_grad: bfloat16 [2, 512, 32768], P('tmpl', 'row', 'col'), may hold values from -6 to 6
- in_gain: float32 [64], replicated, may hold values from 0.25 to 1.75
- out_gain: float32 [64], replicated, may hold values from 0.25 to 1.75
- w_in: bfloat16 [64, 320], replicated, may hold values from -0.75 to 0.75
- w_out: bfloat16 [64, 64], replicated, may hold values from -0.75 to 0.75
Outputs:
- trunk_grad: float32 [512, 32768], P(('row', 'tmpl'), 'col')
All inputs are finite; a program needn't handle non-finite values.
Results may differ from a plain program's by a relative error of at most 0.0067.
Values may be sent and summed in bfloat16 or wider, within the bound.
No kernel may reach another device: no remote copies, remote signals or barrier semaphores. Data moves between devices by JAX's collectives and lax.ppermute only.
A program may use at most 64 MiB of HBM per device.

v0:
```python
import jax
import jax.numpy as jnp
from jax import lax
from jax.sharding import PartitionSpec as P

EPSILON = 1e-05


def normalize(values, gain):
    centre = values - jnp.mean(values, axis=-1, keepdims=True)
    inv_std = lax.rsqrt(jnp.mean(centre * centre, axis=-1, keepdims=True) + EPSILON)
    unit = centre * inv_std
    return (unit * gain, unit, inv_std)


def norm_back(cotangent, unit, inv_std, gain):
    scaled = cotangent * gain
    centred = scaled - jnp.mean(scaled, axis=-1, keepdims=True)
    return (centred - unit * jnp.mean(scaled * unit, axis=-1, keepdims=True)) * inv_std


def gated_pair(projected, channels):
    left = jax.nn.sigmoid(projected[:, :channels]) * projected[:, channels : 2 * channels]
    right = (
        jax.nn.sigmoid(projected[:, 2 * channels : 3 * channels])
        * projected[:, 3 * channels : 4 * channels]
    )
    return (left.astype(jnp.bfloat16), right.astype(jnp.bfloat16))


def gate_grads(projected, d_left, d_right, upstream, mixed_out, out_gate, channels):
    pieces = []
    for offset, d_term in ((0, d_left), (2, d_right)):
        sig_gate = jax.nn.sigmoid(projected[:, offset * channels : (offset + 1) * channels])
        linear = projected[:, (offset + 1) * channels : (offset + 2) * channels]
        pieces.append(d_term * linear * sig_gate * (1.0 - sig_gate))
        pieces.append(d_term * sig_gate)
    pieces.append(upstream * mixed_out * out_gate * (1.0 - out_gate))
    return jnp.concatenate(pieces, axis=-1).astype(jnp.bfloat16)


def turn_tile(tile):
    tile_rows, merged = tile.shape
    sectioned = tile.reshape(1, 1, tile_rows, merged)
    first_move = lax.all_to_all(sectioned, "row", split_axis=3, concat_axis=0, tiled=True)
    second_move = lax.all_to_all(first_move, "col", split_axis=0, concat_axis=1, tiled=True)
    final_move = lax.all_to_all(second_move, "row", split_axis=1, concat_axis=3, tiled=True)
    return final_move.reshape(tile_rows, merged)


def body(pair, saved_product, out_grad, in_gain, out_gain, w_in, w_out):
    channels = in_gain.shape[0]
    tile_rows = pair.shape[1]
    merged = pair.shape[2]
    tile_cols = merged // channels
    normed, in_unit, in_inv = normalize(pair[0].reshape(-1, channels).astype(jnp.float32), in_gain)
    projected = jnp.dot(normed.astype(jnp.bfloat16), w_in, preferred_element_type=jnp.float32)
    left, right = gated_pair(projected, channels)
    left_panel, right_panel = (
        lax.all_gather(left.reshape(tile_rows, merged), "row", axis=0, tiled=True),
        lax.all_gather(right.reshape(tile_rows, merged), "row", axis=0, tiled=True),
    )
    left_panel = left_panel.reshape(-1, tile_cols, channels)
    right_panel = right_panel.reshape(-1, tile_cols, channels)
    out_norm, out_unit, out_inv = normalize(
        saved_product[0].reshape(-1, channels).astype(jnp.float32), out_gain
    )
    mixed_out = jnp.dot(out_norm.astype(jnp.bfloat16), w_out, preferred_element_type=jnp.float32)
    upstream = out_grad[0].reshape(-1, channels).astype(jnp.float32)
    out_gate = jax.nn.sigmoid(projected[:, 4 * channels :])
    d_mixed = (upstream * out_gate).astype(jnp.bfloat16)
    d_norm = jnp.dot(d_mixed, w_out.T, preferred_element_type=jnp.float32)
    d_product = (
        norm_back(d_norm, out_unit, out_inv, out_gain)
        .astype(jnp.bfloat16)
        .reshape(tile_rows, merged)
    )
    piece = lax.all_gather(d_product, "col", axis=1, tiled=True)
    count = piece.shape[1] // channels
    d_left = jnp.einsum(
        "ijc,jkc->ikc",
        piece.reshape(tile_rows, count, channels),
        right_panel,
        preferred_element_type=jnp.float32,
    )
    turned = turn_tile(d_product)
    piece = lax.all_gather(turned, "col", axis=0, tiled=True)
    count = piece.shape[0]
    d_right = jnp.einsum(
        "ijc,ikc->jkc",
        piece.reshape(count, tile_cols, channels),
        left_panel,
        preferred_element_type=jnp.float32,
    )
    d_proj = gate_grads(
        projected,
        d_left.reshape(-1, channels),
        d_right.reshape(-1, channels),
        upstream,
        mixed_out,
        out_gate,
        channels,
    )
    d_normed = jnp.dot(d_proj, w_in.T, preferred_element_type=jnp.float32)
    pair_grad = norm_back(d_normed, in_unit, in_inv, in_gain).reshape(tile_rows, merged)
    return lax.psum_scatter(pair_grad, "tmpl", scatter_dimension=0, tiled=True)


def solution(mesh):
    in_specs = (
        P("tmpl", "row", "col"),
        P("tmpl", "row", "col"),
        P("tmpl", "row", "col"),
        P(),
        P(),
        P(),
        P(),
    )
    out_specs = P(("row", "tmpl"), "col")
    return jax.shard_map(body, mesh=mesh, in_specs=in_specs, out_specs=out_specs, check_vma=False)
```

profile of v0, /device:TPU:1, one launch (start us, length us, event | category | flops | bytes accessed | tf_op | source)
XLA Modules:
  0.0 336.8 jit_solution(14726945253524920972)
XLA Ops:
  6.5 1.1 reshape.112
  8.1 1.1 reshape.114
  11.2 0.9 reshape.103
  12.6 0.9 reshape.101
  13.7 0.9 reshape.106
  15.0 0.7 copy.71
  16.3 11.5 %reduce = bf16[2048,32]{1,0:T(8,128)(2,1)S(1)} reduce(bf16[2048,1,1,32]{3,2,1,0:T(2,128)(2,1)S(1)} %bitcast.39, bf16[]{:T(256)} %broadcast.115), dimensions={1,2}, to_apply=%bitcast.28.reduce_sub_computation | reduce | bytes 262146
  28.3 16.9 %all_to_all.45 = bf16[16,2,2048]{2,1,0:T(2,128)(2,1)S(1)} all-to-all(bf16[16,2,2048]{2,1,0:T(2,128)(2,1)S(1)} %reshape.115), channel_id=1, replica_groups=mesh['tmpl'=2,'row'=16,'col'=16] {'row'}, dimensions={0} | all-to-all | bytes 262144 | tf_op jit(solution)/shard_map/all_to_all | solution.py:45
  45.3 0.7 reshape.116
  46.6 26.2 %all_to_all.46 = bf16[16,1,32,128]{3,2,1,0:T(8,128)(2,1)S(1)} all-to-all(bf16[16,1,32,128]{3,2,1,0:T(8,128)(2,1)S(1)} %copy.73), channel_id=1, replica_groups=mesh['tmpl'=2,'row'=16,'col'=16] {'col'}, dimensions={0} | all-to-all | bytes 262144 | tf_op jit(solution)/shard_map/all_to_all | solution.py:46
  72.8 14.2 %all_to_all.47 = bf16[1,16,32,128]{3,2,0,1:T(8,128)(2,1)S(1)} all-to-all(bf16[1,16,32,128]{3,2,0,1:T(8,128)(2,1)S(1)} %bitcast.47), channel_id=1, replica_groups=mesh['tmpl'=2,'row'=16,'col'=16] {'row'}, dimensions={1} | all-to-all | bytes 262144 | tf_op jit(solution)/shard_map/all_to_all | solution.py:47
  87.1 0.7 copy.99
  88.0 6.5 %reshape.104 = bf16[32,512,64]{2,1,0:T(8,128)(2,1)} reshape(bf16[32,32768]{1,0:T(8,128)(2,1)} %all-gather.7.cloned.1.call-done) | data formatting | bytes 4194304 | tf_op jit(solution)/shard_map/reshape | solution.py:82
  94.5 4.7 %copy.64 = bf16[32,512,64]{1,0,2:T(8,128)(2,1)S(1)} copy(bf16[32,512,64]{2,1,0:T(8,128)(2,1)} %reshape.104) | data formatting | bytes 4194304 | tf_op jit(solution)/shard_map/reshape | solution.py:82
  99.2 58.0 %all-gather.5.cloned.1.call-done = bf16[512,2048]{1,0:T(8,128)(2,1)} async-done(((bf16[32,2048]{1,0:T(8,128)(2,1)}), bf16[512,2048]{1,0:T(8,128)(2,1)}) %all-gather.5.cloned.1.call-update) | async-done | bytes 2097168 | tf_op jit(solution)/shard_map/all_gather | solution.py:61
  157.2 3.9 %copy.59 = bf16[512,2048]{0,1:T(8,128)(2,1)} copy(bf16[512,2048]{1,0:T(8,128)(2,1)} %all-gather.5.cloned.1.call-done) | data formatting | bytes 4194304 | tf_op jit(solution)/shard_map/all_gather | solution.py:61
  161.2 3.9 %fusion.5 = f32[32,32,64]{0,1,2:T(8,128)} fusion(bf16[32,512,64]{1,0,2:T(8,128)(2,1)S(1)} %copy.64, bf16[512,32,64]{0,2,1:T(8,128)(2,1)} %bitcast.37), kind=kOutput, calls=%fused_computation.5 | convolution fusion | flops 67108864 | bytes 4456448 | tf_op jit(solution)/shard_map/ijc,jkc->ikc/dot_general | solution.py:80
  165.1 1.9 copy.65
  167.2 55.2 %all-gather.9.cloned.1.call-done = bf16[512,2048]{1,0:T(8,128)(2,1)} async-done(((bf16[32,2048]{1,0:T(8,128)(2,1)}), bf16[512,2048]{1,0:T(8,128)(2,1)}) %all-gather.9.cloned.1.call-update) | async-done | bytes 2097168 | tf_op jit(solution)/shard_map/all_gather | solution.py:60
  222.4 3.9 %copy.69 = bf16[512,2048]{0,1:T(8,128)(2,1)} copy(bf16[512,2048]{1,0:T(8,128)(2,1)} %all-gather.9.cloned.1.call-done) | data formatting | bytes 4194304 | tf_op jit(solution)/shard_map/all_gather | solution.py:60
  226.3 0.7 fusion.27
  227.1 0.7 fusion.28
  227.8 58.5 %all-gather.11.cloned.1.call-done = bf16[512,2048]{1,0:T(8,128)(2,1)} async-done(((bf16[32,2048]{1,0:T(8,128)(2,1)}), bf16[512,2048]{1,0:T(8,128)(2,1)}) %all-gather.11.cloned.1.call-update) | async-done | bytes 2097168 | tf_op jit(solution)/shard_map/all_gather | solution.py:87
  286.3 3.9 %copy.76 = bf16[512,2048]{0,1:T(8,128)(2,1)} copy(bf16[512,2048]{1,0:T(8,128)(2,1)} %all-gather.11.cloned.1.call-done) | data formatting | bytes 4194304 | tf_op jit(solution)/shard_map/all_gather | solution.py:87
  290.2 4.9 %fusion.8 = f32[32,32,64]{0,1,2:T(8,128)} fusion(bf16[512,32,64]{0,2,1:T(8,128)(2,1)} %bitcast.43, bf16[512,32,64]{0,2,1:T(8,128)(2,1)S(1)} %bitcast.42), kind=kOutput, calls=%fused_computation.6 | convolution fusion | flops 67108864 | bytes 4456448 | tf_op jit(solution)/shard_map/ijc,ikc->jkc/dot_general | solution.py:89
  295.1 2.0 copy.79
  297.3 0.7 fusion.29
  298.1 0.7 fusion.30
  298.8 0.9 fusion.16
  299.7 1.4 fusion.39
  301.4 0.9 reshape.111
  302.3 28.0 %reduce-scatter.2.cloned.1.call-done = f32[16,2048]{1,0:T(8,128)} async-done(((f32[32,2048]{1,0:T(8,128)}), f32[16,2048]{1,0:T(8,128)}) %reduce-scatter.2.cloned.1.call-update) | async-done | bytes 131088 | tf_op jit(solution)/shard_map/reduce_scatter | solution.py:106
  (68 shorter events, 5.7 us)
Async XLA Ops:
  6.5 3.7 %copy-start = (bf16[64,320]{1,0:T(8,128)(2,1)S(1)}, bf16[64,320]{1,0:T(8,128)(2,1)}, u32[]{:S(2)}) copy-start(bf16[64,320]{1,0:T(8,128)(2,1)} %param.12) | copy-start | bytes 122884
  6.5 3.3 copy-start.8
  6.5 81.5 %all-gather.7.cloned.1.call-start = ((), (), s32[]{:S(2)}) async-start(), calls=%async_computation.5 | async-start | bytes 2228224 | tf_op jit(solution)/shard_map/all_gather | solution.py:78
  7.9 2.3 copy-start.1
  8.1 2.1 copy-start.9
  9.4 1.5 copy-start.3
  9.4 1.2 copy-start.10
  9.5 1.2 copy-start.11
  10.3 1.0 copy-start.6
  12.2 145.1 %all-gather.5.cloned.1.call-start = ((), (), s32[]{:S(2)}) async-start(), calls=%async_computation.4 | async-start | bytes 2228224 | tf_op jit(solution)/shard_map/all_gather | solution.py:61
  13.5 208.9 %all-gather.9.cloned.1.call-start = ((), (), s32[]{:S(2)}) async-start(), calls=%async_computation.6 | async-start | bytes 2228224 | tf_op jit(solution)/shard_map/all_gather | solution.py:60
  14.7 271.6 %all-gather.11.cloned.1.call-start = ((), (), s32[]{:S(2)}) async-start(), calls=%async_computation.7 | async-start | bytes 2228224 | tf_op jit(solution)/shard_map/all_gather | solution.py:87
  87.8 242.5 %reduce-scatter.2.cloned.1.call-start = ((), (), s32[]{:S(2)}) async-start(), calls=%async_computation.8 | async-start | bytes 393216 | tf_op jit(solution)/shard_map/reduce_scatter | solution.py:106
  227.8 62.4 %copy-start.5 = (bf16[512,2048]{0,1:T(8,128)(2,1)S(1)}, bf16[512,2048]{0,1:T(8,128)(2,1)}, u32[]{:S(2)}) copy-start(bf16[512,2048]{0,1:T(8,128)(2,1)} %copy.69) | copy-start | bytes 6291460
  295.1 3.7 %copy-start.4 = (f32[1024,64]{0,1:T(8,128)S(1)}, f32[1024,64]{0,1:T(8,128)}, u32[]{:S(2)}) copy-start(f32[1024,64]{0,1:T(8,128)} %copy-done.3) | copy-start | bytes 786436
  295.1 3.7 %copy-start.7 = (f32[1024,64]{0,1:T(8,128)S(1)}, f32[1024,64]{0,1:T(8,128)}, u32[]{:S(2)}) copy-start(f32[1024,64]{0,1:T(8,128)} %copy-done.6) | copy-start | bytes 786436
  297.1 2.6 copy-start.2
Sparse Core Ops, SparseCore 0:
  12.3 71.8 all-gather.6
  87.5 69.6 all-gather.4
  160.6 61.7 all-gather.8
  224.3 61.9 all-gather.10
  302.4 27.8 reduce-scatter.1
where the time goes:
time: 338 us; the launch traced here: 337 us
  waiting for transfers between devices  200 us (59%)
  blocking collectives  57.4 us (17%)
  local copies, waits for them, and re-layouts  38.7 us (11%)
  other arithmetic  15.2 us (4%)
  between operations  13.6 us (4%)
  matrix products  11.7 us (3%)
    all_gather x1, waiting for transfers between devices, body(): piece = lax.all_gather(turned, 'col', axis=0, tiled=True)  58.5 us
    all_gather x1, waiting for transfers between devices, body(): lax.all_gather(right.reshape(tile_rows, merged), 'row', axis=0, tiled=True)  58 us
    all_gather x1, waiting for transfers between devices, body(): lax.all_gather(left.reshape(tile_rows, merged), 'row', axis=0, tiled=True)  55.2 us
    reduce_scatter x1, waiting for transfers between devices, body(): return lax.psum_scatter(pair_grad, 'tmpl', scatter_dimension=0, tiled=True)  28 us
    all_to_all x1, blocking collectives, turn_tile(): lax.all_to_all(first_move, 'col', split_axis=0, concat_axis=1, tiled=True)  26.2 us
    all_to_all x1, blocking collectives, turn_tile(): lax.all_to_all(sectioned, 'row', split_axis=3, concat_axis=0, tiled=True)  16.9 us
    unnamed x5, other arithmetic  14.4 us
    all_to_all x1, blocking collectives, turn_tile(): lax.all_to_all(second_move, 'row', split_axis=1, concat_axis=3, tiled=True)  14.2 us
  transfers between devices with their start and end apart: 5, of which 4 were waited for; matrix products, arithmetic and copies ran while one was open for 13% of the time, Pallas kernels for 0%

commit v1 on v0

v1 whole, which is shorter than its diff:
```python
import jax
import jax.numpy as jnp
from jax import lax
from jax.sharding import PartitionSpec as P

EPSILON = 1e-05
BF16 = jnp.bfloat16
F32 = jnp.float32


def normalize(values, gain):
    centre = values - jnp.mean(values, axis=0, keepdims=True)
    inv_std = lax.rsqrt(jnp.mean(centre * centre, axis=0, keepdims=True) + EPSILON)
    unit = centre * inv_std
    return (unit * gain, unit, inv_std)


def norm_back(cotangent, unit, inv_std, gain):
    scaled = cotangent * gain
    centred = scaled - jnp.mean(scaled, axis=0, keepdims=True)
    return (centred - unit * jnp.mean(scaled * unit, axis=0, keepdims=True)) * inv_std


def channel_major(tile, channels):
    return tile.reshape(-1, channels).T.astype(F32)


def dot(a, b, dims):
    return lax.dot_general(a, b, (dims, ((), ())), preferred_element_type=F32)


def solution(mesh):
    rows_n, cols_n, tmpl_n = mesh.shape["row"], mesh.shape["col"], mesh.shape["tmpl"]

    def body(pair, saved, upstream, in_gain, out_gain, w_in, w_out):
        channels = in_gain.shape[0]
        near = channels // rows_n
        quads = cols_n // near
        pair, saved, upstream = pair[0], saved[0], upstream[0]
        tile_rows, merged = pair.shape
        tile_cols = merged // channels
        half = tile_rows // tmpl_n
        gain_in, gain_out = in_gain[:, None], out_gain[:, None]
        mine = lax.axis_index("tmpl")
        quad = lax.axis_index("col") // near

        both = jnp.concatenate([pair, saved, upstream], axis=0).reshape(3, tmpl_n, half, merged)
        give = lax.dynamic_index_in_dim(both, 1 - mine, 1, keepdims=False)
        keep = lax.dynamic_index_in_dim(both, mine, 1, keepdims=False)
        other = lax.ppermute(give, "tmpl", [(0, 1), (1, 0)])

        def project(pair_cm):
            normed, unit, inv = normalize(pair_cm, gain_in)
            return dot(w_in, normed.astype(BF16), ((0,), (0,))), unit, inv

        proj, _, _ = project(channel_major(pair, channels))
        gate = [proj[n * channels : (n + 1) * channels] for n in range(5)]
        left = (jax.nn.sigmoid(gate[0]) * gate[1]).astype(BF16)
        right = (jax.nn.sigmoid(gate[2]) * gate[3]).astype(BF16)
        _, out_unit, out_inv = normalize(channel_major(saved, channels), gain_out)
        up = channel_major(upstream, channels)
        d_mixed = (up * jax.nn.sigmoid(gate[4])).astype(BF16)
        d_norm = dot(w_out, d_mixed, ((1,), (0,)))
        d_prod = norm_back(d_norm, out_unit, out_inv, gain_out).astype(BF16)

        send = jnp.stack([d_prod, left, right], axis=1).reshape(channels, -1, 128)
        groups = [
            [r * cols_n + near * q + m for r in range(rows_n) for m in range(near)]
            for q in range(quads)
        ]
        got = lax.all_to_all(send, ("row", "col"), 0, 0, axis_index_groups=groups, tiled=True)
        got = got.reshape(rows_n, near, 3, tile_rows, tile_cols).transpose(2, 0, 3, 1, 4)
        got = got.reshape(3, rows_n * tile_rows, near * tile_cols)
        d_own, left_all, right_all = got[0], got[1], got[2]
        width = near * tile_cols
        d_of = [d_own] + [
            lax.ppermute(d_own, "col", [(z, (z - near * s) % cols_n) for z in range(cols_n)])
            for s in range(1, quads)
        ]

        mixed = jnp.concatenate([keep, other], axis=1)
        proj2, in_unit, in_inv = project(channel_major(mixed[0], channels))
        gate2 = [proj2[n * channels : (n + 1) * channels] for n in range(5)]
        normed2, _, _ = normalize(channel_major(mixed[1], channels), gain_out)
        mixed_out = dot(w_out, normed2.astype(BF16), ((0,), (0,)))
        out_gate = jax.nn.sigmoid(gate2[4])
        d_og = (channel_major(mixed[2], channels) * mixed_out * out_gate * (1.0 - out_gate)).astype(BF16)

        right_quads = right_all.reshape(quads, -1, width)
        d_left = jnp.zeros((rows_n * tile_rows, width), F32)
        d_rights = []
        for s in range(quads):
            r_s = lax.dynamic_index_in_dim(right_quads, (quad + s) % quads, 0, keepdims=False)
            d_left = d_left + dot(d_of[s], r_s, ((1,), (0,)))
            d_rights.append(dot(d_of[s], left_all, ((0,), (0,))).astype(BF16))
        twice = jnp.stack(d_rights + d_rights[: quads - 1])
        d_right = lax.dynamic_slice_in_dim(twice, (quads - quad) % quads, quads, 0)
        d_right = d_right.reshape(rows_n * tile_rows, width)
        back = jnp.stack([d_left.astype(BF16), d_right])
        back = back.reshape(2, rows_n, tmpl_n, half, near, tile_cols).transpose(2, 1, 4, 0, 3, 5)
        back = back.reshape(tmpl_n * channels, -1, 128)
        groups = [
            [
                (t * rows_n + r) * cols_n + near * q + m
                for t in range(tmpl_n)
                for r in range(rows_n)
                for m in range(near)
            ]
            for q in range(quads)
        ]
        home = lax.all_to_all(
            back, ("tmpl", "row", "col"), 0, 0, axis_index_groups=groups, tiled=True
        )
        home = home.reshape(tmpl_n, channels, 2, half * tile_cols)
        home = jnp.where(mine == 0, home, home[::-1])
        d_left2, d_right2 = (
            jnp.concatenate([home[0, :, n], home[1, :, n]], axis=1).astype(F32) for n in (0, 1)
        )
        pieces = []
        for d_term, sig, linear in (
            (d_left2, jax.nn.sigmoid(gate2[0]), gate2[1]),
            (d_right2, jax.nn.sigmoid(gate2[2]), gate2[3]),
        ):
            pieces.append((d_term * linear * sig * (1.0 - sig)).astype(BF16))
            pieces.append((d_term * sig).astype(BF16))
        d_proj = jnp.concatenate(pieces + [d_og], axis=0)
        d_normed = dot(w_in, d_proj, ((1,), (0,)))
        grad = norm_back(d_normed, in_unit, in_inv, gain_in)
        cells = half * tile_cols
        grad = grad[:, :cells] + grad[:, cells:]
        return grad.T.reshape(half, merged)

    in_specs = (P("tmpl", "row", "col"),) * 3 + (P(),) * 4
    out_specs = P(("row", "tmpl"), "col")
    return jax.shard_map(body, mesh=mesh, in_specs=in_specs, out_specs=out_specs, check_vma=False)
```

time: 338 us -> 108 us (0.32)
  waiting for transfers between devices: 200 us -> 41 us
  blocking collectives: 57.4 us -> 0 us
  starting transfers between devices: 0.35 us -> 45.2 us
  local copies, waits for them, and re-layouts: 38.7 us -> 14.3 us
  between operations: 13.6 us -> 0.81 us
  other arithmetic: 15.2 us -> 2.75 us
  matrix products: 11.7 us -> 3.17 us
    all_gather x4 -> x0, waiting for transfers between devices: 172 us -> none  [the longest x1 58.5 us: body(): piece = lax.all_gather(turned, 'col', axis=0, tiled=True)]
    all_to_all x3 -> x0, blocking collectives: 57.4 us -> none  [the longest x1 26.2 us: turn_tile(): lax.all_to_all(first_move, 'col', split_axis=0, concat_axis=1, tiled=True)]
    reduce_scatter x1 -> x0, waiting for transfers between devices: 28 us -> none  [body(): return lax.psum_scatter(pair_grad, 'tmpl', scatter_dimension=0, tiled=True)]
    ppermute x0 -> x4, waiting for transfers between devices: none -> 25.9 us  [the longest x3 18.3 us: body(): lax.ppermute(d_own, 'col', [(z, (z - near * s) % cols_n) for z in range(c...]
    ppermute x0 -> x4, starting transfers between devices: none -> 24.2 us  [the longest x3 21.9 us: body(): lax.ppermute(d_own, 'col', [(z, (z - near * s) % cols_n) for z in range(c...]
    all_to_all x0 -> x2, starting transfers between devices: none -> 21 us  [the longest x1 13 us: body(): lax.all_to_all(send, ('row', 'col'), 0, 0, axis_index_groups=groups, tile...]
    all_to_all x0 -> x2, waiting for transfers between devices: none -> 15.1 us  [the longest x1 12.4 us: body(): lax.all_to_all(back, ('tmpl', 'row', 'col'), 0, 0, axis_index_groups=grou...]
    unnamed x5 -> x4, other arithmetic: 14.4 us -> 0.36 us
  transfers between devices with their start and end apart: 5 -> 6, of which waited for: 4 -> 4; matrix products, arithmetic and copies ran while one was open for 13% -> 6% of each run, Pallas kernels for 0% -> 0%
where the time goes in v1:
time: 108 us; the launch traced here: 107 us
  starting transfers between devices  45.2 us (42%)
  waiting for transfers between devices  41 us (38%)
  local copies, waits for them, and re-layouts  14.3 us (13%)
  matrix products  3.17 us (3%)
  other arithmetic  2.75 us (3%)
    ppermute x3, starting transfers between devices, body(): lax.ppermute(d_own, 'col', [(z, (z - near * s) % cols_n) for z in range(c...  21.9 us
    ppermute x3, waiting for transfers between devices, body(): lax.ppermute(d_own, 'col', [(z, (z - near * s) % cols_n) for z in range(c...  18.3 us
    all_to_all x1, starting transfers between devices, body(): lax.all_to_all(send, ('row', 'col'), 0, 0, axis_index_groups=groups, tile...  13 us
    all_to_all x1, waiting for transfers between devices, body(): lax.all_to_all(back, ('tmpl', 'row', 'col'), 0, 0, axis_index_groups=grou...  12.4 us
    all_to_all x1, starting transfers between devices, body(): lax.all_to_all(back, ('tmpl', 'row', 'col'), 0, 0, axis_index_groups=grou...  7.99 us
    ppermute x1, waiting for transfers between devices, body(): other = lax.ppermute(give, 'tmpl', [(0, 1), (1, 0)])  7.58 us
    convert_element_type x12, local copies, waits for them, and re-layouts, channel_major(): return tile.reshape(-1, channels).T.astype(F32)  4.71 us
    dot_general x13, matrix products, dot(): return lax.dot_general(a, b, (dims, ((), ())), preferred_element_type=F32)  3.17 us
  transfers between devices with their start and end apart: 6, of which 4 were waited for; matrix products, arithmetic and copies ran while one was open for 6% of the time, Pallas kernels for 0%

profile of v1, /device:TPU:1, one launch (start us, length us, event | category | flops | bytes accessed | tf_op | source)
XLA Modules:
  0.0 107.2 jit_solution(3463524083728224582)
XLA Ops:
  0.0 1.1 %reshape.114 = f32[1024,64]{1,0:T(8,128)S(1)} reshape(bf16[1,32,2048]{2,1,0:T(8,128)(2,1)} %param.7) | data formatting | bytes 393216 | tf_op jit(solution)/shard_map/convert_element_type | solution.py:25
  2.9 0.4 convolution_bitcast_fusion.1
  4.0 0.3 copy.23
  4.4 1.1 %reshape.108 = bf16[64,24,128]{2,1,0:T(8,128)(2,1)} reshape(bf16[64,3,1024]{2,1,0:T(4,128)(2,1)S(1)} %copy.23) | data formatting | bytes 786432 | tf_op jit(solution)/shard_map/reshape | solution.py:66
  5.4 13.0 %all-to-all-start = ((bf16[64,24,128]{2,1,0:T(8,128)(2,1)}), bf16[64,24,128]{2,1,0:T(8,128)(2,1)S(1)}, u32[]{:S(2)}, u32[]{:S(2)}) async-start(bf16[64,24,128]{2,1,0:T(8,128)(2,1)} %reshape.108), calls=%async_computation | async-start | bytes 786432 | tf_op jit(solution)/shard_map/all_to_all | solution.py:71
  18.6 2.2 %collective-permute-start.3 = (bf16[3,16,2048]{2,1,0:T(8,128)(2,1)S(1)}, bf16[3,16,2048]{2,1,0:T(8,128)(2,1)S(1)}, u32[]{:S(2)}, u32[]{:S(2)}) collective-permute-start(bf16[3,16,2048]{2,1,0:T(8,128)(2,1)S(1)} %get-tuple-element.17), channel_id=1, source_target_pairs={{0,256},{256,0},{1,257},{257,1},{2,258},{258,2},{3,259},{259,3},{4... | collective-permute-start | bytes 589832 | tf_op jit(solution)/shard_map/ppermute | solution.py:50
  20.9 7.6 %collective-permute-done.3 = bf16[3,16,2048]{2,1,0:T(8,128)(2,1)S(1)} collective-permute-done((bf16[3,16,2048]{2,1,0:T(8,128)(2,1)S(1)}, bf16[3,16,2048]{2,1,0:T(8,128)(2,1)S(1)}, u32[]{:S(2)}, u32[]{:S(2)}) %collective-permute-start.3) | collective-permute-done | bytes 196640 | tf_op jit(solution)/shard_map/ppermute | solution.py:50
  29.4 0.9 copy.33
  30.7 0.9 copy.34
  31.7 2.6 %all-to-all-done = bf16[64,24,128]{2,1,0:T(8,128)(2,1)S(1)} async-done(((bf16[64,24,128]{2,1,0:T(8,128)(2,1)}), bf16[64,24,128]{2,1,0:T(8,128)(2,1)S(1)}, u32[]{:S(2)}, u32[]{:S(2)}) %all-to-all-start) | async-done | bytes 393248 | tf_op jit(solution)/shard_map/all_to_all | solution.py:71
  34.3 0.6 reshape.109
  35.0 1.4 %copy.24 = bf16[16,4,3,32,32]{3,0,4,1,2:T(8,128)(2,1)S(1)} copy(bf16[16,4,3,32,32]{4,3,2,1,0:T(8,128)(2,1)S(1)} %reshape.109) | data formatting | bytes 786432 | tf_op jit(solution)/shard_map/reshape | solution.py:72
  36.3 0.3 fusion.74
  36.6 0.4 squeeze.47
  37.1 9.8 %collective-permute-start = (bf16[512,128]{0,1:T(8,128)(2,1)S(1)}, bf16[512,128]{0,1:T(8,128)(2,1)S(1)}, u32[]{:S(2)}, u32[]{:S(2)}) collective-permute-start(bf16[512,128]{0,1:T(8,128)(2,1)S(1)} %squeeze.47), channel_id=1, source_target_pairs={{0,12},{1,13},{2,14},{3,15},{4,0},{5,1},{6,2},{7,3},{8,4},{9,5},{1... | collective-permute-start | bytes 393224 | tf_op jit(solution)/shard_map/ppermute | solution.py:77
  46.8 1.9 %collective-permute-start.2 = (bf16[512,128]{0,1:T(8,128)(2,1)S(1)}, bf16[512,128]{0,1:T(8,128)(2,1)S(1)}, u32[]{:S(2)}, u32[]{:S(2)}) collective-permute-start(bf16[512,128]{0,1:T(8,128)(2,1)S(1)} %squeeze.47), channel_id=1, source_target_pairs={{0,4},{1,5},{2,6},{3,7},{4,8},{5,9},{6,10},{7,11},{8,12},{9,13},{1... | collective-permute-start | bytes 393224 | tf_op jit(solution)/shard_map/ppermute | solution.py:77
  48.8 10.3 %collective-permute-start.1 = (bf16[512,128]{0,1:T(8,128)(2,1)S(1)}, bf16[512,128]{0,1:T(8,128)(2,1)S(1)}, u32[]{:S(2)}, u32[]{:S(2)}) collective-permute-start(bf16[512,128]{0,1:T(8,128)(2,1)S(1)} %squeeze.47), channel_id=1, source_target_pairs={{0,8},{1,9},{2,10},{3,11},{4,12},{5,13},{6,14},{7,15},{8,0},{9,1},... | collective-permute-start | bytes 393224 | tf_op jit(solution)/shard_map/ppermute | solution.py:77
  59.0 0.3 reshape_squeeze.2
  59.3 0.3 constant_dynamic-slice_fusion.2
  60.3 0.5 squeeze.52
  61.4 18.3 %collective-permute-done.1 = bf16[512,128]{0,1:T(8,128)(2,1)S(1)} collective-permute-done((bf16[512,128]{0,1:T(8,128)(2,1)S(1)}, bf16[512,128]{0,1:T(8,128)(2,1)S(1)}, u32[]{:S(2)}, u32[]{:S(2)}) %collective-permute-start.1) | collective-permute-done | bytes 131104 | tf_op jit(solution)/shard_map/ppermute | solution.py:77
  80.0 0.2 stack.42
  80.9 0.2 stack.48
  81.2 0.9 maximum_bitcast_fusion
  82.3 1.2 %reshape.110 = bf16[128,8,128]{2,1,0:T(8,128)(2,1)} reshape(bf16[2,16,4,2,16,32]{5,4,3,2,1,0:T(8,128)(2,1)S(1)} %copy.29) | data formatting | bytes 524288 | tf_op jit(solution)/shard_map/reshape | solution.py:101
  83.5 8.0 %all-to-all-start.1 = ((bf16[128,8,128]{2,1,0:T(8,128)(2,1)}), bf16[128,8,128]{2,1,0:T(8,128)(2,1)S(1)}, u32[]{:S(2)}, u32[]{:S(2)}) async-start(bf16[128,8,128]{2,1,0:T(8,128)(2,1)} %reshape.110), calls=%async_computation.1 | async-start | bytes 524288 | tf_op jit(solution)/shard_map/all_to_all | solution.py:111
  91.6 0.4 convolution_bitcast_fusion
  92.0 12.4 %all-to-all-done.1 = bf16[128,8,128]{2,1,0:T(8,128)(2,1)S(1)} async-done(((bf16[128,8,128]{2,1,0:T(8,128)(2,1)}), bf16[128,8,128]{2,1,0:T(8,128)(2,1)S(1)}, u32[]{:S(2)}, u32[]{:S(2)}) %all-to-all-start.1) | async-done | bytes 262176 | tf_op jit(solution)/shard_map/all_to_all | solution.py:111
  105.0 0.6 copy-done.5
  105.6 0.3 fusion.6
  105.8 0.3 fusion.72
  106.4 0.8 reshape.113
  (82 shorter events, 6.9 us)
Async XLA Ops:
  0.0 2.9 %copy-start = (bf16[64,320]{1,0:T(8,128)(2,1)S(1)}, bf16[64,320]{1,0:T(8,128)(2,1)}, u32[]{:S(2)}) copy-start(bf16[64,320]{1,0:T(8,128)(2,1)} %param.12) | copy-start | bytes 122884
  0.0 1.6 %copy-start.3 = (bf16[1,32,2048]{2,1,0:T(8,128)(2,1)S(1)}, bf16[1,32,2048]{2,1,0:T(8,128)(2,1)}, u32[]{:S(2)}) copy-start(bf16[1,32,2048]{2,1,0:T(8,128)(2,1)} %param.8) | copy-start | bytes 393220
  1.6 0.9 copy-start.2
  2.0 0.9 copy-start.6
  2.9 0.7 copy-start.7
  2.9 0.7 copy-start.8
  4.0 14.5 %copy-start.4 = (bf16[1,32,2048]{2,1,0:T(8,128)(2,1)S(1)}, bf16[1,32,2048]{2,1,0:T(8,128)(2,1)}, u32[]{:S(2)}) copy-start(bf16[1,32,2048]{2,1,0:T(8,128)(2,1)} %param.7) | copy-start | bytes 393220
  5.4 28.9 %all-to-all-start = ((bf16[64,24,128]{2,1,0:T(8,128)(2,1)}), bf16[64,24,128]{2,1,0:T(8,128)(2,1)S(1)}, u32[]{:S(2)}, u32[]{:S(2)}) async-start(bf16[64,24,128]{2,1,0:T(8,128)(2,1)} %reshape.108), calls=%async_computation | async-start | bytes 786432 | tf_op jit(solution)/shard_map/all_to_all | solution.py:71
  18.6 9.9 %collective-permute-start.3 = (bf16[3,16,2048]{2,1,0:T(8,128)(2,1)S(1)}, bf16[3,16,2048]{2,1,0:T(8,128)(2,1)S(1)}, u32[]{:S(2)}, u32[]{:S(2)}) collective-permute-start(bf16[3,16,2048]{2,1,0:T(8,128)(2,1)S(1)} %get-tuple-element.17), channel_id=1, source_target_pairs={{0,256},{256,0},{1,257},{257,1},{2,258},{258,2},{3,259},{259,3},{4... | collective-permute-start | bytes 589832 | tf_op jit(solution)/shard_map/ppermute | solution.py:50
  37.1 23.9 %collective-permute-start = (bf16[512,128]{0,1:T(8,128)(2,1)S(1)}, bf16[512,128]{0,1:T(8,128)(2,1)S(1)}, u32[]{:S(2)}, u32[]{:S(2)}) collective-permute-start(bf16[512,128]{0,1:T(8,128)(2,1)S(1)} %squeeze.47), channel_id=1, source_target_pairs={{0,12},{1,13},{2,14},{3,15},{4,0},{5,1},{6,2},{7,3},{8,4},{9,5},{1... | collective-permute-start | bytes 393224 | tf_op jit(solution)/shard_map/ppermute | solution.py:77
  46.8 14.4 %collective-permute-start.2 = (bf16[512,128]{0,1:T(8,128)(2,1)S(1)}, bf16[512,128]{0,1:T(8,128)(2,1)S(1)}, u32[]{:S(2)}, u32[]{:S(2)}) collective-permute-start(bf16[512,128]{0,1:T(8,128)(2,1)S(1)} %squeeze.47), channel_id=1, source_target_pairs={{0,4},{1,5},{2,6},{3,7},{4,8},{5,9},{6,10},{7,11},{8,12},{9,13},{1... | collective-permute-start | bytes 393224 | tf_op jit(solution)/shard_map/ppermute | solution.py:77
  48.8 31.0 %collective-permute-start.1 = (bf16[512,128]{0,1:T(8,128)(2,1)S(1)}, bf16[512,128]{0,1:T(8,128)(2,1)S(1)}, u32[]{:S(2)}, u32[]{:S(2)}) collective-permute-start(bf16[512,128]{0,1:T(8,128)(2,1)S(1)} %squeeze.47), channel_id=1, source_target_pairs={{0,8},{1,9},{2,10},{3,11},{4,12},{5,13},{6,14},{7,15},{8,0},{9,1},... | collective-permute-start | bytes 393224 | tf_op jit(solution)/shard_map/ppermute | solution.py:77
  82.3 9.2 %copy-start.1 = (f32[1024,64]{0,1:T(8,128)S(1)}, f32[1024,64]{0,1:T(8,128)}, u32[]{:S(2)}) copy-start(f32[1024,64]{0,1:T(8,128)} %copy.33) | copy-start | bytes 786436
  83.5 20.9 %all-to-all-start.1 = ((bf16[128,8,128]{2,1,0:T(8,128)(2,1)}), bf16[128,8,128]{2,1,0:T(8,128)(2,1)S(1)}, u32[]{:S(2)}, u32[]{:S(2)}) async-start(bf16[128,8,128]{2,1,0:T(8,128)(2,1)} %reshape.110), calls=%async_computation.1 | async-start | bytes 524288 | tf_op jit(solution)/shard_map/all_to_all | solution.py:111
  104.6 1.0 copy-start.5

commit v2 on v1

v2 whole, which is shorter than its diff:
```python
import jax
import jax.numpy as jnp
from jax import lax
from jax.experimental import pallas as pl
from jax.experimental.pallas import tpu as pltpu
from jax.sharding import PartitionSpec as P


EPSILON = 1e-05
BF16 = jnp.bfloat16
F32 = jnp.float32
LANES = 128


def normalize(values, gain):
    scale = 1.0 / values.shape[0]
    centre = values - jnp.sum(values, axis=0, keepdims=True) * scale
    inv_std = lax.rsqrt(jnp.sum(centre * centre, axis=0, keepdims=True) * scale + EPSILON)
    unit = centre * inv_std
    return unit * gain, unit, inv_std


def norm_back(cotangent, unit, inv_std, gain):
    scale = 1.0 / cotangent.shape[0]
    scaled = cotangent * gain
    centred = scaled - jnp.sum(scaled, axis=0, keepdims=True) * scale
    return (centred - unit * (jnp.sum(scaled * unit, axis=0, keepdims=True) * scale)) * inv_std


def dot(a, b, dims):
    return lax.dot_general(a, b, (dims, ((), ())), preferred_element_type=F32)


def column(gain_ref):
    gain = gain_ref[...]
    return jnp.broadcast_to(gain, (LANES, gain.shape[1])).T[:, :1]


def turn(rows):
    turned = jnp.concatenate(rows, axis=0).astype(F32).T
    half = turned.shape[0] // 2
    return jnp.concatenate([turned[:half], turned[half:]], axis=1)


def swap_groups(values, lane):
    count = len(values)
    values = list(values)
    bit = count // 2
    while bit:
        shift = bit * (LANES // count)
        low = (lane & shift) == 0
        for v in range(count):
            if v & bit == 0:
                a, b = values[v], values[v + bit]
                values[v] = jnp.where(low, a, pltpu.roll(b, shift, 1))
                values[v + bit] = jnp.where(low, pltpu.roll(a, LANES - shift, 1), b)
        bit //= 2
    return values


def lanes_of(rows):
    return lax.broadcasted_iota(jnp.int32, (rows, LANES), 1)


def spread_kernel(pair, saved, upstream, in_gain, out_gain, w_in, w_out, send, held):
    channels = w_out.shape[0]
    gain_in, gain_out = column(in_gain), column(out_gain)
    weights, weights_out = w_in[...], w_out[...]
    for b in range(4):

        def tile(ref):
            return turn([ref[0, :, (4 * k + b) * LANES : (4 * k + b + 1) * LANES] for k in range(4)])

        normed, _, _ = normalize(tile(pair), gain_in)
        proj = dot(weights, normed.astype(BF16), ((0,), (0,)))
        gate = [proj[n * channels : (n + 1) * channels] for n in range(5)]
        left = jax.nn.sigmoid(gate[0]) * gate[1]
        right = jax.nn.sigmoid(gate[2]) * gate[3]
        _, unit, inv = normalize(tile(saved), gain_out)
        d_mixed = (tile(upstream) * jax.nn.sigmoid(gate[4])).astype(BF16)
        d_norm = dot(weights_out, d_mixed, ((1,), (0,)))
        d_prod = norm_back(d_norm, unit, inv, gain_out)
        for n, value in enumerate((d_prod, left, right)):
            for p in range(2):
                at = (n * 8 + 2 * b + p) * channels
                held[at : at + channels, :] = value[:, p * LANES : (p + 1) * LANES]
    for c in range(channels):
        send[c] = held[pl.ds(c, 24, stride=channels), :].astype(BF16)


def gather_kernel(got, d_own, left_all, right_all):
    lane = lanes_of(8)
    for n, out in enumerate((d_own, left_all, right_all)):
        for m in range(4):
            for block in range(4):
                parts = swap_groups(
                    [
                        got[(4 * block + r) * 4 + m, n * 8 : (n + 1) * 8, :].astype(F32)
                        for r in range(4)
                    ],
                    lane,
                )
                for k in range(2):
                    out[
                        m * 32 + k * 16 : m * 32 + (k + 1) * 16,
                        block * LANES : (block + 1) * LANES,
                    ] = jnp.concatenate(parts[2 * k : 2 * k + 2], axis=0).astype(BF16)


def product_kernel(quad_ref, left_all, right_all, d0, d1, d2, d3, back, d_left, d_right):
    quad = quad_ref[0]
    total = None
    left = left_all[...]
    for s, d_ref in enumerate((d0, d1, d2, d3)):
        at = pl.multiple_of(lax.rem(quad + s, 4) * LANES, LANES)
        d_s = d_ref[...]
        term = dot(right_all[:, pl.ds(at, LANES)], d_s, ((1,), (0,)))
        total = term if total is None else total + term
        d_right[:, pl.ds(at, LANES)] = dot(left, d_s, ((1,), (1,)))
    d_left[...] = total
    lane = lanes_of(8)
    for m in range(4):
        for block in range(4):
            columns = slice(block * LANES, (block + 1) * LANES)
            chunks = swap_groups(
                [
                    ref[m * 32 + k * 8 : m * 32 + (k + 1) * 8, columns]
                    for ref in (d_left, d_right)
                    for k in range(4)
                ],
                lane,
            )
            for u, chunk in enumerate(chunks):
                r, half = block * 4 + u // 2, u % 2
                back[half * 64 + r * 4 + m] = chunk.astype(BF16)


def prepare_kernel(mine_ref, pair, saved, upstream, other, in_gain, out_gain, w_in, w_out, factors, rest, units, invs):
    channels = w_out.shape[0]
    first = pl.multiple_of(mine_ref[0] * 16, 16)
    gain_in, gain_out = column(in_gain), column(out_gain)
    weights, weights_out = w_in[...], w_out[...]
    for b in range(4):

        def tile(n, ref):
            spans = [slice((4 * k + b) * LANES, (4 * k + b + 1) * LANES) for k in range(4)]
            return turn(
                [ref[0, pl.ds(first, 16), span] for span in spans]
                + [other[n, :, span] for span in spans]
            )

        span = slice(2 * b * LANES, (2 * b + 2) * LANES)
        normed, unit, inv = normalize(tile(0, pair), gain_in)
        units[:, span], invs[:, span] = unit, inv
        proj = dot(weights, normed.astype(BF16), ((0,), (0,)))
        gate = [proj[n * channels : (n + 1) * channels] for n in range(5)]
        for n in range(2):
            sig, linear = jax.nn.sigmoid(gate[2 * n]), gate[2 * n + 1]
            factors[2 * n, :, span] = linear * sig * (1.0 - sig)
            factors[2 * n + 1, :, span] = sig
        normed, _, _ = normalize(tile(1, saved), gain_out)
        mixed = dot(weights_out, normed.astype(BF16), ((0,), (0,)))
        out_gate = jax.nn.sigmoid(gate[4])
        d_og = (tile(2, upstream) * mixed * out_gate * (1.0 - out_gate)).astype(BF16)
        rest[:, span] = dot(weights[:, 4 * channels :], d_og, ((1,), (0,)))


def finish_kernel(mine_ref, home, factors, rest, units, invs, in_gain, w_in, out, held):
    channels = rest.shape[0]
    mine = mine_ref[0]
    gain_in = column(in_gain)
    weights = w_in[:, : 4 * channels]
    for t in range(2):
        base = lax.rem(mine + t, 2) * channels
        for c in range(channels):
            at = (t * channels + c) * 8
            held[at : at + 8, :] = home[base + c].astype(F32)
    low = lanes_of(channels) < LANES // 2
    for b in range(4):
        sums = []
        for p in range(2):
            g = 2 * b + p
            span = slice(g * LANES, (g + 1) * LANES)
            h0 = held[pl.ds(g, channels, stride=8), :]
            h1 = held[pl.ds(8 * channels + g, channels, stride=8), :]
            d_left = jnp.where(low, h0, pltpu.roll(h1, LANES // 2, 1))
            d_right = jnp.where(low, pltpu.roll(h0, LANES // 2, 1), h1)
            d_proj = jnp.concatenate(
                [
                    (d * factors[n, :, span]).astype(BF16)
                    for n, d in enumerate((d_left, d_left, d_right, d_right))
                ],
                axis=0,
            )
            d_normed = dot(weights, d_proj, ((1,), (0,))) + rest[:, span]
            grad = norm_back(d_normed, units[:, span], invs[:, span], gain_in)
            sums.append(grad + pltpu.roll(grad, LANES // 2, 1))
        turned = jnp.concatenate(sums, axis=0).T
        for k in range(4):
            out[:, (4 * k + b) * LANES : (4 * k + b + 1) * LANES] = turned[k * 16 : (k + 1) * 16]


def shaped(dims, kind):
    return jax.ShapeDtypeStruct(dims, kind)


VMEM = pl.BlockSpec(memory_space=pltpu.VMEM)
SMEM = pl.BlockSpec(memory_space=pltpu.SMEM)


def call(kernel, outs, args, scratch=(), scalars=0, cost=1, limit=16):
    return pl.pallas_call(
        kernel,
        out_shape=outs,
        in_specs=[SMEM] * scalars + [VMEM] * (len(args) - scalars),
        out_specs=jax.tree.map(lambda _: VMEM, outs),
        scratch_shapes=list(scratch),
        compiler_params=pltpu.CompilerParams(vmem_limit_bytes=limit * 2**20),
        cost_estimate=pl.CostEstimate(
            flops=cost * 10**8, bytes_accessed=cost * 10**6, transcendentals=0
        ),
    )(*args)


def solution(mesh):
    rows_n, cols_n, tmpl_n = mesh.shape["row"], mesh.shape["col"], mesh.shape["tmpl"]

    def body(pair, saved, upstream, in_gain, out_gain, w_in, w_out):
        channels = in_gain.shape[0]
        near = channels // rows_n
        quads = cols_n // near
        _, tile_rows, merged = pair.shape
        half = tile_rows // tmpl_n
        in_gain, out_gain = in_gain[None], out_gain[None]
        mine = lax.axis_index("tmpl")
        quad = lax.axis_index("col") // near
        mine1, quad1 = mine[None].astype(jnp.int32), quad[None].astype(jnp.int32)
        cells = tile_rows * merged // channels
        count = cells // LANES

        give = jnp.concatenate(
            [
                lax.dynamic_slice_in_dim(x, (1 - mine) * half, half, 1)
                for x in (pair, saved, upstream)
            ],
            axis=0,
        )
        other = lax.ppermute(give, "tmpl", [(0, 1), (1, 0)])

        send = call(
            spread_kernel,
            shaped((channels, 3 * count, LANES), BF16),
            (pair, saved, upstream, in_gain, out_gain, w_in, w_out),
            scratch=[pltpu.VMEM((channels * 3 * count, LANES), F32)],
            limit=60,
        )
        groups = [
            [r * cols_n + near * q + m for r in range(rows_n) for m in range(near)]
            for q in range(quads)
        ]
        got = lax.all_to_all(send, ("row", "col"), 0, 0, axis_index_groups=groups, tiled=True)
        panel = shaped((LANES, rows_n * tile_rows), BF16)
        d_own, left_all, right_all = call(gather_kernel, (panel,) * 3, (got,))
        far = {}
        for s in (2, 1, 3):
            far[s] = lax.ppermute(
                d_own, "col", [(z, (z - near * s) % cols_n) for z in range(cols_n)]
            )

        factors, rest, units, invs = call(
            prepare_kernel,
            (
                shaped((4, channels, cells), F32),
                shaped((channels, cells), F32),
                shaped((channels, cells), F32),
                shaped((1, cells), F32),
            ),
            (mine1, pair, saved, upstream, other, in_gain, out_gain, w_in, w_out),
            scalars=1,
        )

        back = call(
            product_kernel,
            shaped((tmpl_n * channels, count, LANES), BF16),
            (quad1, left_all, right_all, d_own, far[1], far[2], far[3]),
            scratch=[pltpu.VMEM((LANES, rows_n * tile_rows), F32)] * 2,
            scalars=1,
        )
        groups = [
            [
                (t * rows_n + r) * cols_n + near * q + m
                for t in range(tmpl_n)
                for r in range(rows_n)
                for m in range(near)
            ]
            for q in range(quads)
        ]
        home = lax.all_to_all(
            back, ("tmpl", "row", "col"), 0, 0, axis_index_groups=groups, tiled=True
        )
        return call(
            finish_kernel,
            shaped((half, merged), F32),
            (mine1, home, factors, rest, units, invs, in_gain, w_in),
            scratch=[pltpu.VMEM((tmpl_n * channels * count, LANES), F32)],
            scalars=1,
        )

    in_specs = (P("tmpl", "row", "col"),) * 3 + (P(),) * 4
    out_specs = P(("row", "tmpl"), "col")
    return jax.shard_map(body, mesh=mesh, in_specs=in_specs, out_specs=out_specs, check_vma=False)
```

time: 108 us -> 96.4 us (0.89)
  blocking collectives: 0 us -> 28.9 us
  waiting for transfers between devices: 41 us -> 25.3 us
  starting transfers between devices: 45.2 us -> 31.4 us
  local copies, waits for them, and re-layouts: 14.3 us -> 0.91 us
  Pallas kernels: 0 us -> 9.33 us
  matrix products: 3.17 us -> 0 us
  other arithmetic: 2.75 us -> 0.03 us
    all_to_all x0 -> x1, blocking collectives: none -> 28.9 us  [body(): lax.all_to_all(send, ('row', 'col'), 0, 0, axis_index_groups=groups, tile...]
    all_to_all x1 -> x0, starting transfers between devices: 13 us -> none  [body(): lax.all_to_all(send, ('row', 'col'), 0, 0, axis_index_groups=groups, tile...]
    all_to_all x1, waiting for transfers between devices: 12.4 us -> 1.51 us  [body(): lax.all_to_all(back, ('tmpl', 'row', 'col'), 0, 0, axis_index_groups=grou...]
    pallas_call x0 -> x5, Pallas kernels: none -> 9.33 us  [call(): pl.pallas_call(kernel, out_shape=outs, in_specs=[SMEM] * scalars + [VMEM]...]
    reshape x7 -> x0, local copies, waits for them, and re-layouts: 5.22 us -> none  [the longest x2 2.02 us: body(): got.reshape(rows_n, near, 3, tile_rows, tile_cols).transpose(2, 0, 3, 1, 4)]
    convert_element_type x12 -> x0, local copies, waits for them, and re-layouts: 4.71 us -> none  [channel_major(): return tile.reshape(-1, channels).T.astype(F32)]
    dot_general x13 -> x0, matrix products: 3.17 us -> none  [dot(): return lax.dot_general(a, b, (dims, ((), ())), preferred_element_type=F32)]
    all_to_all x1 -> x0, waiting for transfers between devices: 2.62 us -> none  [body(): lax.all_to_all(send, ('row', 'col'), 0, 0, axis_index_groups=groups, tile...]
  transfers between devices with their start and end apart: 6 -> 5, of which waited for: 4 -> 4; matrix products, arithmetic and copies ran while one was open for 6% -> 0% of each run, Pallas kernels for 0% -> 1%
where the time goes in v2:
time: 96.4 us; the launch traced here: 96 us
  starting transfers between devices  31.4 us (33%)
  blocking collectives  28.9 us (30%)
  waiting for transfers between devices  25.3 us (26%)
  Pallas kernels  9.33 us (10%)
    all_to_all x1, blocking collectives, body(): lax.all_to_all(send, ('row', 'col'), 0, 0, axis_index_groups=groups, tile...  28.9 us
    ppermute x3, starting transfers between devices, body(): lax.ppermute(d_own, 'col', [(z, (z - near * s) % cols_n) for z in range(c...  21.9 us
    ppermute x3, waiting for transfers between devices, body(): lax.ppermute(d_own, 'col', [(z, (z - near * s) % cols_n) for z in range(c...  18.2 us
    pallas_call x5, Pallas kernels, call(): pl.pallas_call(kernel, out_shape=outs, in_specs=[SMEM] * scalars + [VMEM]...  9.33 us
    all_to_all x1, starting transfers between devices, body(): lax.all_to_all(back, ('tmpl', 'row', 'col'), 0, 0, axis_index_groups=grou...  5.8 us
    ppermute x1, waiting for transfers between devices, body(): other = lax.ppermute(give, 'tmpl', [(0, 1), (1, 0)])  5.53 us
    ppermute x1, starting transfers between devices, body(): other = lax.ppermute(give, 'tmpl', [(0, 1), (1, 0)])  3.7 us
  transfers between devices with their start and end apart: 5, of which 4 were waited for; matrix products, arithmetic and copies ran while one was open for 0% of the time, Pallas kernels for 1%

profile of v2, /device:TPU:1, one launch (start us, length us, event | category | flops | bytes accessed | tf_op | source)
XLA Modules:
  0.0 96.0 jit_solution(8171010309563032297)
XLA Ops:
  0.0 3.4 %shard_map.73 = bf16[64,24,128]{2,1,0:T(8,128)(2,1)} custom-call(bf16[1,32,2048]{2,1,0:T(8,128)(2,1)} %pair.3, bf16[1,32,2048]{2,1,0:T(8,128)(2,1)} %saved.3, bf16[1,32,2048]{2,1,0:T(8,128)(2,1)} %upstream.3, f32[1,64]{1,0:T(1,128)} %bitcast.4, f32[1,64]{1,0:T(1,128)} %bitcast.7, bf16[64,320]{1,0:T(8,128)(2,1)} %w_in.5, bf16[64,64]{1,0:T(8,128)(2,1)} %w_out.3), custom_call_target="tpu_custom_call" | custom-call | flops 100000000 | bytes 1000000 | tf_op jit(solution)/shard_map/pallas_call | solution.py:212
  3.4 28.9 %all_to_all.10.got = bf16[64,24,128]{2,1,0:T(8,128)(2,1)S(1)} all-to-all(bf16[64,24,128]{2,1,0:T(8,128)(2,1)} %shard_map.73), channel_id=1, replica_groups={{0,1,2,3,16,17,18,19,32,33,34,35,48,49,50,51,64,65,66,67,80,81,82,83,96..., dimensions={0} | all-to-all | bytes 786432 | tf_op jit(solution)/shard_map/all_to_all | solution.py:261
  32.3 1.9 %shard_map.74 = (bf16[128,512]{1,0:T(8,128)(2,1)S(1)}, bf16[128,512]{1,0:T(8,128)(2,1)S(1)}, bf16[128,512]{1,0:T(8,128)(2,1)S(1)}) custom-call(bf16[64,24,128]{2,1,0:T(8,128)(2,1)S(1)} %all_to_all.10.got), custom_call_target="tpu_custom_call" | custom-call | flops 100000000 | bytes 1000000 | tf_op jit(solution)/shard_map/pallas_call | solution.py:212
  34.2 8.8 %collective-permute-start.2 = (bf16[128,512]{1,0:T(8,128)(2,1)S(1)}, bf16[128,512]{1,0:T(8,128)(2,1)S(1)}, u32[]{:S(2)}, u32[]{:S(2)}) collective-permute-start(bf16[128,512]{1,0:T(8,128)(2,1)S(1)} %get-tuple-element.14.d0), channel_id=1, source_target_pairs={{0,4},{1,5},{2,6},{3,7},{4,8},{5,9},{6,10},{7,11},{8,12},{9,13},{1... | collective-permute-start | bytes 393224 | tf_op jit(solution)/shard_map/ppermute | solution.py:266
  43.0 7.9 %collective-permute-start.1 = (bf16[128,512]{1,0:T(8,128)(2,1)S(1)}, bf16[128,512]{1,0:T(8,128)(2,1)S(1)}, u32[]{:S(2)}, u32[]{:S(2)}) collective-permute-start(bf16[128,512]{1,0:T(8,128)(2,1)S(1)} %get-tuple-element.14.d0), channel_id=1, source_target_pairs={{0,8},{1,9},{2,10},{3,11},{4,12},{5,13},{6,14},{7,15},{8,0},{9,1},... | collective-permute-start | bytes 393224 | tf_op jit(solution)/shard_map/ppermute | solution.py:266
  51.0 5.2 %collective-permute-start = (bf16[128,512]{1,0:T(8,128)(2,1)S(1)}, bf16[128,512]{1,0:T(8,128)(2,1)S(1)}, u32[]{:S(2)}, u32[]{:S(2)}) collective-permute-start(bf16[128,512]{1,0:T(8,128)(2,1)S(1)} %get-tuple-element.14.d0), channel_id=1, source_target_pairs={{0,12},{1,13},{2,14},{3,15},{4,0},{5,1},{6,2},{7,3},{8,4},{9,5},{1... | collective-permute-start | bytes 393224 | tf_op jit(solution)/shard_map/ppermute | solution.py:266
  56.2 0.0 collective-permute-done.2.d3
  56.2 11.2 %collective-permute-done.1.d2 = bf16[128,512]{1,0:T(8,128)(2,1)S(1)} collective-permute-done((bf16[128,512]{1,0:T(8,128)(2,1)S(1)}, bf16[128,512]{1,0:T(8,128)(2,1)S(1)}, u32[]{:S(2)}, u32[]{:S(2)}) %collective-permute-start.1) | collective-permute-done | bytes 131104 | tf_op jit(solution)/shard_map/ppermute | solution.py:266
  67.3 7.1 %collective-permute-done.d1 = bf16[128,512]{1,0:T(8,128)(2,1)S(1)} collective-permute-done((bf16[128,512]{1,0:T(8,128)(2,1)S(1)}, bf16[128,512]{1,0:T(8,128)(2,1)S(1)}, u32[]{:S(2)}, u32[]{:S(2)}) %collective-permute-start) | collective-permute-done | bytes 131104 | tf_op jit(solution)/shard_map/ppermute | solution.py:266
  74.4 1.5 %shard_map.75 = bf16[128,8,128]{2,1,0:T(8,128)(2,1)} custom-call(s32[1]{0:T(128)} %bitcast.1.quad_ref, bf16[128,512]{1,0:T(8,128)(2,1)S(1)} %get-tuple-element.12.left_all, bf16[128,512]{1,0:T(8,128)(2,1)S(1)} %get-tuple-element.13.right_all, bf16[128,512]{1,0:T(8,128)(2,1)S(1)} %get-tuple-element.14.d0, bf16[128,512]{1,0:T(8,128)(2,1)S(1)} %collective-permute-done.d1, ...), custom_call_target="tpu_custom_call" | custom-call | flops 100000000 | bytes 1000000 | tf_op jit(solution)/shard_map/pallas_call | solution.py:212
  75.9 0.0 copy-start
  75.9 0.0 copy-start.2
  75.9 5.8 %all-to-all-start.1 = ((bf16[128,8,128]{2,1,0:T(8,128)(2,1)}), bf16[128,8,128]{2,1,0:T(8,128)(2,1)S(1)}, u32[]{:S(2)}, u32[]{:S(2)}) async-start(bf16[128,8,128]{2,1,0:T(8,128)(2,1)} %shard_map.75), calls=%async_computation.1 | async-start | bytes 524288 | tf_op jit(solution)/shard_map/all_to_all | solution.py:298
  81.7 0.0 copy-start.1
  81.7 0.0 copy-done
  81.8 0.0 copy-done.2
  81.8 0.8 copy-done.1
  82.6 0.0 copy-start.3
  82.6 0.0 copy-start.4
  82.7 0.0 copy-start.5
  82.7 0.0 copy-start.6
  82.7 3.7 %collective-permute-start.3 = (bf16[3,16,2048]{2,1,0:T(8,128)(2,1)S(1)}, bf16[3,16,2048]{2,1,0:T(8,128)(2,1)S(1)}, u32[]{:S(2)}, u32[]{:S(2)}) collective-permute-start(bf16[3,16,2048]{2,1,0:T(8,128)(2,1)S(1)} %pad_maximum_fusion), channel_id=1, source_target_pairs={{0,256},{256,0},{1,257},{257,1},{2,258},{258,2},{3,259},{259,3},{4... | collective-permute-start | bytes 589832 | tf_op jit(solution)/shard_map/ppermute | solution.py:248
  86.4 5.5 %collective-permute-done.3.other = bf16[3,16,2048]{2,1,0:T(8,128)(2,1)S(1)} collective-permute-done((bf16[3,16,2048]{2,1,0:T(8,128)(2,1)S(1)}, bf16[3,16,2048]{2,1,0:T(8,128)(2,1)S(1)}, u32[]{:S(2)}, u32[]{:S(2)}) %collective-permute-start.3) | collective-permute-done | bytes 196640 | tf_op jit(solution)/shard_map/ppermute | solution.py:248
  91.9 0.0 copy-done.3
  91.9 0.0 copy-done.4
  92.0 0.0 copy-done.5
  92.0 0.0 copy-done.6
  92.0 1.2 %shard_map.76 = (f32[4,64,1024]{2,1,0:T(8,128)S(1)}, f32[64,1024]{1,0:T(8,128)S(1)}, f32[64,1024]{1,0:T(8,128)S(1)}, f32[1,1024]{1,0:T(1,128)S(1)}) custom-call(s32[1]{0:T(128)} %bitcast.mine_ref, bf16[1,32,2048]{2,1,0:T(8,128)(2,1)S(1)} %copy-done, bf16[1,32,2048]{2,1,0:T(8,128)(2,1)S(1)} %copy-done.1, bf16[1,32,2048]{2,1,0:T(8,128)(2,1)S(1)} %copy-done.2, ...), custom_call_target="tpu_custom_call" | custom-call | flops 100000000 | bytes 1000000 | tf_op jit(solution)/shard_map/pallas_call | solution.py:212
  93.2 1.5 %all-to-all-done.1.home = bf16[128,8,128]{2,1,0:T(8,128)(2,1)S(1)} async-done(((bf16[128,8,128]{2,1,0:T(8,128)(2,1)}), bf16[128,8,128]{2,1,0:T(8,128)(2,1)S(1)}, u32[]{:S(2)}, u32[]{:S(2)}) %all-to-all-start.1) | async-done | bytes 262176 | tf_op jit(solution)/shard_map/all_to_all | solution.py:298
  94.7 1.3 %shard_map.77 = f32[16,2048]{1,0:T(8,128)} custom-call(s32[1]{0:T(128)} %bitcast.mine_ref, bf16[128,8,128]{2,1,0:T(8,128)(2,1)S(1)} %all-to-all-done.1.home, f32[4,64,1024]{2,1,0:T(8,128)S(1)} %get-tuple-element.15.factors, f32[64,1024]{1,0:T(8,128)S(1)} %get-tuple-element.16.rest, f32[64,1024]{1,0:T(8,128)S(1)} %get-tuple-element.17.units, ...), custom_call_target="tpu_custom_call" | custom-call | flops 100000000 | bytes 1000000 | tf_op jit(solution)/shard_map/pallas_call | solution.py:212
  (3 shorter events, 0.0 us)
Async XLA Ops:
  34.2 22.0 %collective-permute-start.2 = (bf16[128,512]{1,0:T(8,128)(2,1)S(1)}, bf16[128,512]{1,0:T(8,128)(2,1)S(1)}, u32[]{:S(2)}, u32[]{:S(2)}) collective-permute-start(bf16[128,512]{1,0:T(8,128)(2,1)S(1)} %get-tuple-element.14.d0), channel_id=1, source_target_pairs={{0,4},{1,5},{2,6},{3,7},{4,8},{5,9},{6,10},{7,11},{8,12},{9,13},{1... | collective-permute-start | bytes 393224 | tf_op jit(solution)/shard_map/ppermute | solution.py:266
  43.0 24.3 %collective-permute-start.1 = (bf16[128,512]{1,0:T(8,128)(2,1)S(1)}, bf16[128,512]{1,0:T(8,128)(2,1)S(1)}, u32[]{:S(2)}, u32[]{:S(2)}) collective-permute-start(bf16[128,512]{1,0:T(8,128)(2,1)S(1)} %get-tuple-element.14.d0), channel_id=1, source_target_pairs={{0,8},{1,9},{2,10},{3,11},{4,12},{5,13},{6,14},{7,15},{8,0},{9,1},... | collective-permute-start | bytes 393224 | tf_op jit(solution)/shard_map/ppermute | solution.py:266
  51.0 23.4 %collective-permute-start = (bf16[128,512]{1,0:T(8,128)(2,1)S(1)}, bf16[128,512]{1,0:T(8,128)(2,1)S(1)}, u32[]{:S(2)}, u32[]{:S(2)}) collective-permute-start(bf16[128,512]{1,0:T(8,128)(2,1)S(1)} %get-tuple-element.14.d0), channel_id=1, source_target_pairs={{0,12},{1,13},{2,14},{3,15},{4,0},{5,1},{6,2},{7,3},{8,4},{9,5},{1... | collective-permute-start | bytes 393224 | tf_op jit(solution)/shard_map/ppermute | solution.py:266
  75.9 5.8 %copy-start = (bf16[1,32,2048]{2,1,0:T(8,128)(2,1)S(1)}, bf16[1,32,2048]{2,1,0:T(8,128)(2,1)}, u32[]{:S(2)}) copy-start(bf16[1,32,2048]{2,1,0:T(8,128)(2,1)} %pair.3) | copy-start | bytes 393220
  75.9 5.9 %copy-start.2 = (bf16[1,32,2048]{2,1,0:T(8,128)(2,1)S(1)}, bf16[1,32,2048]{2,1,0:T(8,128)(2,1)}, u32[]{:S(2)}) copy-start(bf16[1,32,2048]{2,1,0:T(8,128)(2,1)} %upstream.3) | copy-start | bytes 393220
  75.9 18.8 %all-to-all-start.1 = ((bf16[128,8,128]{2,1,0:T(8,128)(2,1)}), bf16[128,8,128]{2,1,0:T(8,128)(2,1)S(1)}, u32[]{:S(2)}, u32[]{:S(2)}) async-start(bf16[128,8,128]{2,1,0:T(8,128)(2,1)} %shard_map.75), calls=%async_computation.1 | async-start | bytes 524288 | tf_op jit(solution)/shard_map/all_to_all | solution.py:298
  81.7 0.9 copy-start.1
  82.6 9.3 %copy-start.3 = (bf16[64,320]{1,0:T(8,128)(2,1)S(1)}, bf16[64,320]{1,0:T(8,128)(2,1)}, u32[]{:S(2)}) copy-start(bf16[64,320]{1,0:T(8,128)(2,1)} %w_in.5) | copy-start | bytes 122884
  82.6 9.3 %copy-start.4 = (bf16[64,64]{1,0:T(8,128)(2,1)S(1)}, bf16[64,64]{1,0:T(8,128)(2,1)}, u32[]{:S(2)}) copy-start(bf16[64,64]{1,0:T(8,128)(2,1)} %w_out.3) | copy-start | bytes 24580
  82.7 9.3 %copy-start.5 = (f32[64]{0:T(128)S(1)}, f32[64]{0:T(128)}, u32[]{:S(2)}) copy-start(f32[64]{0:T(128)} %param.10) | copy-start | bytes 772
  82.7 9.3 %copy-start.6 = (f32[64]{0:T(128)S(1)}, f32[64]{0:T(128)}, u32[]{:S(2)}) copy-start(f32[64]{0:T(128)} %param.11) | copy-start | bytes 772
  82.7 9.2 %collective-permute-start.3 = (bf16[3,16,2048]{2,1,0:T(8,128)(2,1)S(1)}, bf16[3,16,2048]{2,1,0:T(8,128)(2,1)S(1)}, u32[]{:S(2)}, u32[]{:S(2)}) collective-permute-start(bf16[3,16,2048]{2,1,0:T(8,128)(2,1)S(1)} %pad_maximum_fusion), channel_id=1, source_target_pairs={{0,256},{256,0},{1,257},{257,1},{2,258},{258,2},{3,259},{259,3},{4... | collective-permute-start | bytes 589832 | tf_op jit(solution)/shard_map/ppermute | solution.py:248

commit v3 on v2

--- a/solution.py
+++ b/solution.py
@@ -62,7 +62,17 @@
     return lax.broadcasted_iota(jnp.int32, (rows, LANES), 1)
 
 
-def spread_kernel(pair, saved, upstream, in_gain, out_gain, w_in, w_out, send, held):
+def spread_kernel(*refs):
+    given, send, copies, held, arrived = refs[:7], refs[7], refs[8:15], refs[15], refs[16]
+    moves = [
+        pltpu.make_async_copy(src, dst, arrived.at[n])
+        for n, (src, dst) in enumerate(zip(given, copies))
+    ]
+    for move in moves:
+        move.start()
+    for n in (3, 4, 5, 6, 0, 1, 2):
+        moves[n].wait()
+    pair, saved, upstream, in_gain, out_gain, w_in, w_out = copies
     channels = w_out.shape[0]
     gain_in, gain_out = column(in_gain), column(out_gain)
     weights, weights_out = w_in[...], w_out[...]
@@ -88,23 +98,37 @@
         send[c] = held[pl.ds(c, 24, stride=channels), :].astype(BF16)
 
 
-def gather_kernel(got, d_own, left_all, right_all):
+def collect(got, n, lane):
+    for m in range(4):
+        for block in range(4):
+            parts = swap_groups(
+                [
+                    got[(4 * block + r) * 4 + m, n * 8 : (n + 1) * 8, :].astype(F32)
+                    for r in range(4)
+                ],
+                lane,
+            )
+            for k in range(2):
+                yield (
+                    m * 32 + k * 16,
+                    slice(block * LANES, (block + 1) * LANES),
+                    jnp.concatenate(parts[2 * k : 2 * k + 2], axis=0).astype(BF16),
+                )
+
+
+def cotangent_kernel(got, out):
+    for row, columns, value in collect(got, 0, lanes_of(8)):
+        out[row : row + 16, columns] = value
+
+
+def operand_kernel(mine_ref, got, pair, saved, upstream, left_all, right_all, give):
     lane = lanes_of(8)
-    for n, out in enumerate((d_own, left_all, right_all)):
-        for m in range(4):
-            for block in range(4):
-                parts = swap_groups(
-                    [
-                        got[(4 * block + r) * 4 + m, n * 8 : (n + 1) * 8, :].astype(F32)
-                        for r in range(4)
-                    ],
-                    lane,
-                )
-                for k in range(2):
-                    out[
-                        m * 32 + k * 16 : m * 32 + (k + 1) * 16,
-                        block * LANES : (block + 1) * LANES,
-                    ] = jnp.concatenate(parts[2 * k : 2 * k + 2], axis=0).astype(BF16)
+    first = pl.multiple_of((1 - mine_ref[0]) * 16, 16)
+    for n, ref in enumerate((pair, saved, upstream)):
+        give[n] = ref[0, pl.ds(first, 16), :]
+    for n, out in ((1, left_all), (2, right_all)):
+        for row, columns, value in collect(got, n, lane):
+            out[row : row + 16, columns] = value
 
 
 def product_kernel(quad_ref, left_all, right_all, d0, d1, d2, d3, back, d_left, d_right):
@@ -206,13 +230,14 @@
 
 VMEM = pl.BlockSpec(memory_space=pltpu.VMEM)
 SMEM = pl.BlockSpec(memory_space=pltpu.SMEM)
-
-
-def call(kernel, outs, args, scratch=(), scalars=0, cost=1, limit=16):
+HBM = pl.BlockSpec(memory_space=pltpu.HBM)
+
+
+def call(kernel, outs, args, scratch=(), scalars=0, cost=1, limit=16, space=VMEM):
     return pl.pallas_call(
         kernel,
         out_shape=outs,
-        in_specs=[SMEM] * scalars + [VMEM] * (len(args) - scalars),
+        in_specs=[SMEM] * scalars + [space] * (len(args) - scalars),
         out_specs=jax.tree.map(lambda _: VMEM, outs),
         scratch_shapes=list(scratch),
         compiler_params=pltpu.CompilerParams(vmem_limit_bytes=limit * 2**20),
@@ -238,21 +263,18 @@
         cells = tile_rows * merged // channels
         count = cells // LANES
 
-        give = jnp.concatenate(
-            [
-                lax.dynamic_slice_in_dim(x, (1 - mine) * half, half, 1)
-                for x in (pair, saved, upstream)
-            ],
-            axis=0,
-        )
-        other = lax.ppermute(give, "tmpl", [(0, 1), (1, 0)])
-
+        given = (pair, saved, upstream, in_gain, out_gain, w_in, w_out)
         send = call(
             spread_kernel,
             shaped((channels, 3 * count, LANES), BF16),
-            (pair, saved, upstream, in_gain, out_gain, w_in, w_out),
-            scratch=[pltpu.VMEM((channels * 3 * count, LANES), F32)],
+            given,
+            scratch=[pltpu.VMEM(x.shape, x.dtype) for x in given]
+            + [
+                pltpu.VMEM((channels * 3 * count, LANES), F32),
+                pltpu.SemaphoreType.DMA((len(given),)),
+            ],
             limit=60,
+            space=HBM,
         )
         groups = [
             [r * cols_n + near * q + m for r in range(rows_n) for m in range(near)]
@@ -260,7 +282,14 @@
         ]
         got = lax.all_to_all(send, ("row", "col"), 0, 0, axis_index_groups=groups, tiled=True)
         panel = shaped((LANES, rows_n * tile_rows), BF16)
-        d_own, left_all, right_all = call(gather_kernel, (panel,) * 3, (got,))
+        d_own = call(cotangent_kernel, panel, (got,))
+        left_all, right_all, give = call(
+            operand_kernel,
+            (panel, panel, shaped((3, half, merged), BF16)),
+            (mine1, got, pair, saved, upstream),
+            scalars=1,
+        )
+        other = lax.ppermute(give, "tmpl", [(0, 1), (1, 0)])
         far = {}
         for s in (2, 1, 3):
             far[s] = lax.ppermute(

time: 96.4 us -> 94.7 us (0.982)
  Pallas kernels: 9.33 us -> 8.35 us
    pallas_call x5 -> x6, Pallas kernels: 9.33 us -> 8.35 us  [call(): pl.pallas_call(kernel, out_shape=outs, in_specs=[SMEM] * scalars + [space...]
  transfers between devices with their start and end apart: 5 -> 5, of which waited for: 4 -> 4; matrix products, arithmetic and copies ran while one was open for 0% -> 0% of each run, Pallas kernels for 1% -> 2%
where the time goes in v3:
time: 94.7 us; the launch traced here: 94.3 us
  starting transfers between devices  31.4 us (33%)
  blocking collectives  28.9 us (31%)
  waiting for transfers between devices  25.4 us (27%)
  Pallas kernels  8.35 us (9%)
    all_to_all x1, blocking collectives, body(): lax.all_to_all(send, ('row', 'col'), 0, 0, axis_index_groups=groups, tile...  28.9 us
    ppermute x3, starting transfers between devices, body(): lax.ppermute(d_own, 'col', [(z, (z - near * s) % cols_n) for z in range(c...  21.9 us
    ppermute x3, waiting for transfers between devices, body(): lax.ppermute(d_own, 'col', [(z, (z - near * s) % cols_n) for z in range(c...  17.4 us
    pallas_call x6, Pallas kernels, call(): pl.pallas_call(kernel, out_shape=outs, in_specs=[SMEM] * scalars + [space...  8.35 us
    ppermute x1, waiting for transfers between devices, body(): other = lax.ppermute(give, 'tmpl', [(0, 1), (1, 0)])  6.1 us
    all_to_all x1, starting transfers between devices, body(): lax.all_to_all(back, ('tmpl', 'row', 'col'), 0, 0, axis_index_groups=grou...  5.8 us
    ppermute x1, starting transfers between devices, body(): other = lax.ppermute(give, 'tmpl', [(0, 1), (1, 0)])  3.7 us
    all_to_all x1, waiting for transfers between devices, body(): lax.all_to_all(back, ('tmpl', 'row', 'col'), 0, 0, axis_index_groups=grou...  1.92 us
  transfers between devices with their start and end apart: 5, of which 4 were waited for; matrix products, arithmetic and copies ran while one was open for 0% of the time, Pallas kernels for 2%

profile of v3, /device:TPU:1, one launch (start us, length us, event | category | flops | bytes accessed | tf_op | source)
XLA Modules:
  0.0 94.3 jit_solution(12002472061603298503)
XLA Ops:
  0.0 3.4 %shard_map.73 = bf16[64,24,128]{2,1,0:T(8,128)(2,1)} custom-call(bf16[1,32,2048]{2,1,0:T(8,128)(2,1)} %pair.3, bf16[1,32,2048]{2,1,0:T(8,128)(2,1)} %saved.3, bf16[1,32,2048]{2,1,0:T(8,128)(2,1)} %upstream.3, f32[1,64]{1,0:T(1,128)} %bitcast.4, f32[1,64]{1,0:T(1,128)} %bitcast.7, bf16[64,320]{1,0:T(8,128)(2,1)} %w_in.3, bf16[64,64]{1,0:T(8,128)(2,1)} %w_out.1), custom_call_target="tpu_custom_call" | custom-call | flops 100000000 | bytes 1000000 | tf_op jit(solution)/shard_map/pallas_call | solution.py:237
  3.4 28.9 %all_to_all.10.got = bf16[64,24,128]{2,1,0:T(8,128)(2,1)S(1)} all-to-all(bf16[64,24,128]{2,1,0:T(8,128)(2,1)} %shard_map.73), channel_id=1, replica_groups={{0,1,2,3,16,17,18,19,32,33,34,35,48,49,50,51,64,65,66,67,80,81,82,83,96..., dimensions={0} | all-to-all | bytes 786432 | tf_op jit(solution)/shard_map/all_to_all | solution.py:283
  32.3 0.0 copy-start
  32.3 0.0 copy-start.1
  32.3 0.0 copy-start.2
  32.3 0.2 shard_map.75.d0
  32.5 8.8 %collective-permute-start.2 = (bf16[128,512]{1,0:T(8,128)(2,1)S(1)}, bf16[128,512]{1,0:T(8,128)(2,1)S(1)}, u32[]{:S(2)}, u32[]{:S(2)}) collective-permute-start(bf16[128,512]{1,0:T(8,128)(2,1)S(1)} %shard_map.75.d0), channel_id=1, source_target_pairs={{0,4},{1,5},{2,6},{3,7},{4,8},{5,9},{6,10},{7,11},{8,12},{9,13},{1... | collective-permute-start | bytes 393224 | tf_op jit(solution)/shard_map/ppermute | solution.py:295
  41.3 7.9 %collective-permute-start.1 = (bf16[128,512]{1,0:T(8,128)(2,1)S(1)}, bf16[128,512]{1,0:T(8,128)(2,1)S(1)}, u32[]{:S(2)}, u32[]{:S(2)}) collective-permute-start(bf16[128,512]{1,0:T(8,128)(2,1)S(1)} %shard_map.75.d0), channel_id=1, source_target_pairs={{0,8},{1,9},{2,10},{3,11},{4,12},{5,13},{6,14},{7,15},{8,0},{9,1},... | collective-permute-start | bytes 393224 | tf_op jit(solution)/shard_map/ppermute | solution.py:295
  49.2 5.2 %collective-permute-start = (bf16[128,512]{1,0:T(8,128)(2,1)S(1)}, bf16[128,512]{1,0:T(8,128)(2,1)S(1)}, u32[]{:S(2)}, u32[]{:S(2)}) collective-permute-start(bf16[128,512]{1,0:T(8,128)(2,1)S(1)} %shard_map.75.d0), channel_id=1, source_target_pairs={{0,12},{1,13},{2,14},{3,15},{4,0},{5,1},{6,2},{7,3},{8,4},{9,5},{1... | collective-permute-start | bytes 393224 | tf_op jit(solution)/shard_map/ppermute | solution.py:295
  54.5 0.0 copy-done
  54.5 0.0 copy-done.1
  54.5 0.0 copy-done.2
  54.5 0.8 shard_map.74
  55.3 0.0 collective-permute-done.2.d3
  55.3 10.3 %collective-permute-done.1.d2 = bf16[128,512]{1,0:T(8,128)(2,1)S(1)} collective-permute-done((bf16[128,512]{1,0:T(8,128)(2,1)S(1)}, bf16[128,512]{1,0:T(8,128)(2,1)S(1)}, u32[]{:S(2)}, u32[]{:S(2)}) %collective-permute-start.1) | collective-permute-done | bytes 131104 | tf_op jit(solution)/shard_map/ppermute | solution.py:295
  65.6 7.1 %collective-permute-done.d1 = bf16[128,512]{1,0:T(8,128)(2,1)S(1)} collective-permute-done((bf16[128,512]{1,0:T(8,128)(2,1)S(1)}, bf16[128,512]{1,0:T(8,128)(2,1)S(1)}, u32[]{:S(2)}, u32[]{:S(2)}) %collective-permute-start) | collective-permute-done | bytes 131104 | tf_op jit(solution)/shard_map/ppermute | solution.py:295
  72.7 1.5 %shard_map.76 = bf16[128,8,128]{2,1,0:T(8,128)(2,1)} custom-call(s32[1]{0:T(128)} %bitcast.1.quad_ref, bf16[128,512]{1,0:T(8,128)(2,1)S(1)} %get-tuple-element.12.left_all, bf16[128,512]{1,0:T(8,128)(2,1)S(1)} %get-tuple-element.13.right_all, bf16[128,512]{1,0:T(8,128)(2,1)S(1)} %shard_map.75.d0, bf16[128,512]{1,0:T(8,128)(2,1)S(1)} %collective-permute-done.d1, ...), custom_call_target="tpu_custom_call" | custom-call | flops 100000000 | bytes 1000000 | tf_op jit(solution)/shard_map/pallas_call | solution.py:237
  74.2 0.0 copy-start.3
  74.2 0.0 copy-start.4
  74.2 5.8 %all-to-all-start.1 = ((bf16[128,8,128]{2,1,0:T(8,128)(2,1)}), bf16[128,8,128]{2,1,0:T(8,128)(2,1)S(1)}, u32[]{:S(2)}, u32[]{:S(2)}) async-start(bf16[128,8,128]{2,1,0:T(8,128)(2,1)} %shard_map.76), calls=%async_computation.1 | async-start | bytes 524288 | tf_op jit(solution)/shard_map/all_to_all | solution.py:327
  80.0 0.0 copy-start.5
  80.0 0.0 copy-start.6
  80.0 3.7 %collective-permute-start.3 = (bf16[3,16,2048]{2,1,0:T(8,128)(2,1)S(1)}, bf16[3,16,2048]{2,1,0:T(8,128)(2,1)S(1)}, u32[]{:S(2)}, u32[]{:S(2)}) collective-permute-start(bf16[3,16,2048]{2,1,0:T(8,128)(2,1)S(1)} %get-tuple-element.14), channel_id=1, source_target_pairs={{0,256},{256,0},{1,257},{257,1},{2,258},{258,2},{3,259},{259,3},{4... | collective-permute-start | bytes 589832 | tf_op jit(solution)/shard_map/ppermute | solution.py:292
  83.7 6.1 %collective-permute-done.3.other = bf16[3,16,2048]{2,1,0:T(8,128)(2,1)S(1)} collective-permute-done((bf16[3,16,2048]{2,1,0:T(8,128)(2,1)S(1)}, bf16[3,16,2048]{2,1,0:T(8,128)(2,1)S(1)}, u32[]{:S(2)}, u32[]{:S(2)}) %collective-permute-start.3) | collective-permute-done | bytes 196640 | tf_op jit(solution)/shard_map/ppermute | solution.py:292
  89.8 0.0 copy-done.3
  89.8 0.0 copy-done.4
  89.8 0.0 copy-done.5
  89.8 0.0 copy-done.6
  89.8 1.2 %shard_map.77 = (f32[4,64,1024]{2,1,0:T(8,128)S(1)}, f32[64,1024]{1,0:T(8,128)S(1)}, f32[64,1024]{1,0:T(8,128)S(1)}, f32[1,1024]{1,0:T(1,128)S(1)}) custom-call(s32[1]{0:T(128)} %bitcast.mine_ref, bf16[1,32,2048]{2,1,0:T(8,128)(2,1)S(1)} %copy-done, bf16[1,32,2048]{2,1,0:T(8,128)(2,1)S(1)} %copy-done.1, bf16[1,32,2048]{2,1,0:T(8,128)(2,1)S(1)} %copy-done.2, ...), custom_call_target="tpu_custom_call" | custom-call | flops 100000000 | bytes 1000000 | tf_op jit(solution)/shard_map/pallas_call | solution.py:237
  91.1 1.9 %all-to-all-done.1.home = bf16[128,8,128]{2,1,0:T(8,128)(2,1)S(1)} async-done(((bf16[128,8,128]{2,1,0:T(8,128)(2,1)}), bf16[128,8,128]{2,1,0:T(8,128)(2,1)S(1)}, u32[]{:S(2)}, u32[]{:S(2)}) %all-to-all-start.1) | async-done | bytes 262176 | tf_op jit(solution)/shard_map/all_to_all | solution.py:327
  93.0 1.2 %shard_map.78 = f32[16,2048]{1,0:T(8,128)} custom-call(s32[1]{0:T(128)} %bitcast.mine_ref, bf16[128,8,128]{2,1,0:T(8,128)(2,1)S(1)} %all-to-all-done.1.home, f32[4,64,1024]{2,1,0:T(8,128)S(1)} %get-tuple-element.15.factors, f32[64,1024]{1,0:T(8,128)S(1)} %get-tuple-element.16.rest, f32[64,1024]{1,0:T(8,128)S(1)} %get-tuple-element.17.units, ...), custom_call_target="tpu_custom_call" | custom-call | flops 100000000 | bytes 1000000 | tf_op jit(solution)/shard_map/pallas_call | solution.py:237
Async XLA Ops:
  32.3 22.2 %copy-start = (bf16[1,32,2048]{2,1,0:T(8,128)(2,1)S(1)}, bf16[1,32,2048]{2,1,0:T(8,128)(2,1)}, u32[]{:S(2)}) copy-start(bf16[1,32,2048]{2,1,0:T(8,128)(2,1)} %pair.3) | copy-start | bytes 393220
  32.3 22.2 %copy-start.1 = (bf16[1,32,2048]{2,1,0:T(8,128)(2,1)S(1)}, bf16[1,32,2048]{2,1,0:T(8,128)(2,1)}, u32[]{:S(2)}) copy-start(bf16[1,32,2048]{2,1,0:T(8,128)(2,1)} %saved.3) | copy-start | bytes 393220
  32.3 22.2 %copy-start.2 = (bf16[1,32,2048]{2,1,0:T(8,128)(2,1)S(1)}, bf16[1,32,2048]{2,1,0:T(8,128)(2,1)}, u32[]{:S(2)}) copy-start(bf16[1,32,2048]{2,1,0:T(8,128)(2,1)} %upstream.3) | copy-start | bytes 393220
  32.5 22.8 %collective-permute-start.2 = (bf16[128,512]{1,0:T(8,128)(2,1)S(1)}, bf16[128,512]{1,0:T(8,128)(2,1)S(1)}, u32[]{:S(2)}, u32[]{:S(2)}) collective-permute-start(bf16[128,512]{1,0:T(8,128)(2,1)S(1)} %shard_map.75.d0), channel_id=1, source_target_pairs={{0,4},{1,5},{2,6},{3,7},{4,8},{5,9},{6,10},{7,11},{8,12},{9,13},{1... | collective-permute-start | bytes 393224 | tf_op jit(solution)/shard_map/ppermute | solution.py:295
  41.3 24.3 %collective-permute-start.1 = (bf16[128,512]{1,0:T(8,128)(2,1)S(1)}, bf16[128,512]{1,0:T(8,128)(2,1)S(1)}, u32[]{:S(2)}, u32[]{:S(2)}) collective-permute-start(bf16[128,512]{1,0:T(8,128)(2,1)S(1)} %shard_map.75.d0), channel_id=1, source_target_pairs={{0,8},{1,9},{2,10},{3,11},{4,12},{5,13},{6,14},{7,15},{8,0},{9,1},... | collective-permute-start | bytes 393224 | tf_op jit(solution)/shard_map/ppermute | solution.py:295
  49.2 23.4 %collective-permute-start = (bf16[128,512]{1,0:T(8,128)(2,1)S(1)}, bf16[128,512]{1,0:T(8,128)(2,1)S(1)}, u32[]{:S(2)}, u32[]{:S(2)}) collective-permute-start(bf16[128,512]{1,0:T(8,128)(2,1)S(1)} %shard_map.75.d0), channel_id=1, source_target_pairs={{0,12},{1,13},{2,14},{3,15},{4,0},{5,1},{6,2},{7,3},{8,4},{9,5},{1... | collective-permute-start | bytes 393224 | tf_op jit(solution)/shard_map/ppermute | solution.py:295
  74.2 15.6 %copy-start.3 = (bf16[64,320]{1,0:T(8,128)(2,1)S(1)}, bf16[64,320]{1,0:T(8,128)(2,1)}, u32[]{:S(2)}) copy-start(bf16[64,320]{1,0:T(8,128)(2,1)} %w_in.3) | copy-start | bytes 122884
  74.2 15.6 %copy-start.4 = (bf16[64,64]{1,0:T(8,128)(2,1)S(1)}, bf16[64,64]{1,0:T(8,128)(2,1)}, u32[]{:S(2)}) copy-start(bf16[64,64]{1,0:T(8,128)(2,1)} %w_out.1) | copy-start | bytes 24580
  74.2 18.8 %all-to-all-start.1 = ((bf16[128,8,128]{2,1,0:T(8,128)(2,1)}), bf16[128,8,128]{2,1,0:T(8,128)(2,1)S(1)}, u32[]{:S(2)}, u32[]{:S(2)}) async-start(bf16[128,8,128]{2,1,0:T(8,128)(2,1)} %shard_map.76), calls=%async_computation.1 | async-start | bytes 524288 | tf_op jit(solution)/shard_map/all_to_all | solution.py:327
  80.0 9.8 %copy-start.5 = (f32[64]{0:T(128)S(1)}, f32[64]{0:T(128)}, u32[]{:S(2)}) copy-start(f32[64]{0:T(128)} %param.10) | copy-start | bytes 772
  80.0 9.8 %copy-start.6 = (f32[64]{0:T(128)S(1)}, f32[64]{0:T(128)}, u32[]{:S(2)}) copy-start(f32[64]{0:T(128)} %param.11) | copy-start | bytes 772
  80.0 9.8 %collective-permute-start.3 = (bf16[3,16,2048]{2,1,0:T(8,128)(2,1)S(1)}, bf16[3,16,2048]{2,1,0:T(8,128)(2,1)S(1)}, u32[]{:S(2)}, u32[]{:S(2)}) collective-permute-start(bf16[3,16,2048]{2,1,0:T(8,128)(2,1)S(1)} %get-tuple-element.14), channel_id=1, source_target_pairs={{0,256},{256,0},{1,257},{257,1},{2,258},{258,2},{3,259},{259,3},{4... | collective-permute-start | bytes 589832 | tf_op jit(solution)/shard_map/ppermute | solution.py:292

commit v4 on v3

--- a/solution.py
+++ b/solution.py
@@ -63,7 +63,8 @@
 
 
 def spread_kernel(*refs):
-    given, send, copies, held, arrived = refs[:7], refs[7], refs[8:15], refs[15], refs[16]
+    given, send, copies = refs[:7], refs[7], refs[8:15]
+    held, staged, arrived, sent = refs[15:]
     moves = [
         pltpu.make_async_copy(src, dst, arrived.at[n])
         for n, (src, dst) in enumerate(zip(given, copies))
@@ -76,26 +77,47 @@
     channels = w_out.shape[0]
     gain_in, gain_out = column(in_gain), column(out_gain)
     weights, weights_out = w_in[...], w_out[...]
+
+    def tiles(ref):
+        return jnp.concatenate(
+            [
+                turn([ref[0, :, (4 * k + b) * LANES : (4 * k + b + 1) * LANES] for k in range(4)])
+                for b in range(4)
+            ],
+            axis=1,
+        )
+
+    def hold(n, first, value):
+        for g in range(value.shape[1] // LANES):
+            for c in range(channels // 8):
+                at = ((c * 3 + n) * 8 + first + g) * 8
+                held[at : at + 8, :] = value[8 * c : 8 * c + 8, g * LANES : (g + 1) * LANES]
+
+    normed = normalize(tiles(pair), gain_in)[0].astype(BF16)
+    _, unit, inv = normalize(tiles(saved), gain_out)
+    up = tiles(upstream)
+    mixed = []
     for b in range(4):
-
-        def tile(ref):
-            return turn([ref[0, :, (4 * k + b) * LANES : (4 * k + b + 1) * LANES] for k in range(4)])
-
-        normed, _, _ = normalize(tile(pair), gain_in)
-        proj = dot(weights, normed.astype(BF16), ((0,), (0,)))
+        span = slice(2 * b * LANES, (2 * b + 2) * LANES)
+        proj = dot(weights, normed[:, span], ((0,), (0,)))
         gate = [proj[n * channels : (n + 1) * channels] for n in range(5)]
-        left = jax.nn.sigmoid(gate[0]) * gate[1]
-        right = jax.nn.sigmoid(gate[2]) * gate[3]
-        _, unit, inv = normalize(tile(saved), gain_out)
-        d_mixed = (tile(upstream) * jax.nn.sigmoid(gate[4])).astype(BF16)
-        d_norm = dot(weights_out, d_mixed, ((1,), (0,)))
-        d_prod = norm_back(d_norm, unit, inv, gain_out)
-        for n, value in enumerate((d_prod, left, right)):
-            for p in range(2):
-                at = (n * 8 + 2 * b + p) * channels
-                held[at : at + channels, :] = value[:, p * LANES : (p + 1) * LANES]
-    for c in range(channels):
-        send[c] = held[pl.ds(c, 24, stride=channels), :].astype(BF16)
+        hold(1, 2 * b, jax.nn.sigmoid(gate[0]) * gate[1])
+        hold(2, 2 * b, jax.nn.sigmoid(gate[2]) * gate[3])
+        mixed.append((up[:, span] * jax.nn.sigmoid(gate[4])).astype(BF16))
+    d_norm = dot(weights_out, jnp.concatenate(mixed, axis=1), ((1,), (0,)))
+    hold(0, 0, norm_back(d_norm, unit, inv, gain_out))
+    leaves = []
+    for c in range(channels // 8):
+        for u in range(8):
+            for n in range(3):
+                staged[8 * c + u, 8 * n : 8 * n + 8] = held[
+                    pl.ds((c * 3 + n) * 64 + u, 8, stride=8), :
+                ].astype(BF16)
+        rows = pl.ds(8 * c, 8)
+        leaves.append(pltpu.make_async_copy(staged.at[rows], send.at[rows], sent.at[c]))
+        leaves[-1].start()
+    for leave in leaves:
+        leave.wait()
 
 
 def collect(got, n, lane):
@@ -136,7 +158,7 @@
     total = None
     left = left_all[...]
     for s, d_ref in enumerate((d0, d1, d2, d3)):
-        at = pl.multiple_of(lax.rem(quad + s, 4) * LANES, LANES)
+        at = pl.multiple_of(lax.bitwise_xor(quad, s) * LANES, LANES)
         d_s = d_ref[...]
         term = dot(right_all[:, pl.ds(at, LANES)], d_s, ((1,), (0,)))
         total = term if total is None else total + term
@@ -200,25 +222,27 @@
             at = (t * channels + c) * 8
             held[at : at + 8, :] = home[base + c].astype(F32)
     low = lanes_of(channels) < LANES // 2
+    d_lefts, d_rights = [], []
+    for g in range(8):
+        h0 = held[pl.ds(g, channels, stride=8), :]
+        h1 = held[pl.ds(8 * channels + g, channels, stride=8), :]
+        d_lefts.append(jnp.where(low, h0, pltpu.roll(h1, LANES // 2, 1)))
+        d_rights.append(jnp.where(low, pltpu.roll(h0, LANES // 2, 1), h1))
+    d_left, d_right = jnp.concatenate(d_lefts, axis=1), jnp.concatenate(d_rights, axis=1)
+    d_proj = jnp.concatenate(
+        [
+            (d * factors[n]).astype(BF16)
+            for n, d in enumerate((d_left, d_left, d_right, d_right))
+        ],
+        axis=0,
+    )
+    d_normed = dot(weights, d_proj, ((1,), (0,))) + rest[...]
+    grad = norm_back(d_normed, units[...], invs[...], gain_in)
     for b in range(4):
         sums = []
         for p in range(2):
-            g = 2 * b + p
-            span = slice(g * LANES, (g + 1) * LANES)
-            h0 = held[pl.ds(g, channels, stride=8), :]
-            h1 = held[pl.ds(8 * channels + g, channels, stride=8), :]
-            d_left = jnp.where(low, h0, pltpu.roll(h1, LANES // 2, 1))
-            d_right = jnp.where(low, pltpu.roll(h0, LANES // 2, 1), h1)
-            d_proj = jnp.concatenate(
-                [
-                    (d * factors[n, :, span]).astype(BF16)
-                    for n, d in enumerate((d_left, d_left, d_right, d_right))
-                ],
-                axis=0,
-            )
-            d_normed = dot(weights, d_proj, ((1,), (0,))) + rest[:, span]
-            grad = norm_back(d_normed, units[:, span], invs[:, span], gain_in)
-            sums.append(grad + pltpu.roll(grad, LANES // 2, 1))
+            part = grad[:, (2 * b + p) * LANES : (2 * b + p + 1) * LANES]
+            sums.append(part + pltpu.roll(part, LANES // 2, 1))
         turned = jnp.concatenate(sums, axis=0).T
         for k in range(4):
             out[:, (4 * k + b) * LANES : (4 * k + b + 1) * LANES] = turned[k * 16 : (k + 1) * 16]
@@ -233,12 +257,12 @@
 HBM = pl.BlockSpec(memory_space=pltpu.HBM)
 
 
-def call(kernel, outs, args, scratch=(), scalars=0, cost=1, limit=16, space=VMEM):
+def call(kernel, outs, args, scratch=(), scalars=0, cost=1, limit=16, space=VMEM, out_space=VMEM):
     return pl.pallas_call(
         kernel,
         out_shape=outs,
         in_specs=[SMEM] * scalars + [space] * (len(args) - scalars),
-        out_specs=jax.tree.map(lambda _: VMEM, outs),
+        out_specs=jax.tree.map(lambda _: out_space, outs),
         scratch_shapes=list(scratch),
         compiler_params=pltpu.CompilerParams(vmem_limit_bytes=limit * 2**20),
         cost_estimate=pl.CostEstimate(
@@ -271,10 +295,13 @@
             scratch=[pltpu.VMEM(x.shape, x.dtype) for x in given]
             + [
                 pltpu.VMEM((channels * 3 * count, LANES), F32),
+                pltpu.VMEM((channels, 3 * count, LANES), BF16),
                 pltpu.SemaphoreType.DMA((len(given),)),
+                pltpu.SemaphoreType.DMA((channels // 8,)),
             ],
             limit=60,
             space=HBM,
+            out_space=HBM,
         )
         groups = [
             [r * cols_n + near * q + m for r in range(rows_n) for m in range(near)]
@@ -293,7 +320,7 @@
         far = {}
         for s in (2, 1, 3):
             far[s] = lax.ppermute(
-                d_own, "col", [(z, (z - near * s) % cols_n) for z in range(cols_n)]
+                d_own, "col", [(z, z ^ (near * s)) for z in range(cols_n)]
             )
 
         factors, rest, units, invs = call(

time: 94.7 us -> 96.3 us (1.017)
  waiting for transfers between devices: 25.4 us -> 28.1 us
    ppermute x3, starting transfers between devices: 21.9 us -> 18.7 us  [body(): lax.ppermute(d_own, 'col', [(z, z ^ near * s) for z in range(cols_n)])]
    all_to_all x1, starting transfers between devices: 5.8 us -> 8.83 us  [body(): lax.all_to_all(back, ('tmpl', 'row', 'col'), 0, 0, axis_index_groups=grou...]
    ppermute x3, waiting for transfers between devices: 17.4 us -> 20 us  [body(): lax.ppermute(d_own, 'col', [(z, z ^ near * s) for z in range(cols_n)])]
where the time goes in v4:
time: 96.3 us; the launch traced here: 95.9 us
  starting transfers between devices  31.2 us (32%)
  blocking collectives  28.9 us (30%)
  waiting for transfers between devices  28.1 us (29%)
  Pallas kernels  7.56 us (8%)
    all_to_all x1, blocking collectives, body(): lax.all_to_all(send, ('row', 'col'), 0, 0, axis_index_groups=groups, tile...  28.9 us
    ppermute x3, waiting for transfers between devices, body(): lax.ppermute(d_own, 'col', [(z, z ^ near * s) for z in range(cols_n)])  20 us
    ppermute x3, starting transfers between devices, body(): lax.ppermute(d_own, 'col', [(z, z ^ near * s) for z in range(cols_n)])  18.7 us
    all_to_all x1, starting transfers between devices, body(): lax.all_to_all(back, ('tmpl', 'row', 'col'), 0, 0, axis_index_groups=grou...  8.83 us
    pallas_call x6, Pallas kernels, call(): pl.pallas_call(kernel, out_shape=outs, in_specs=[SMEM] * scalars + [space...  7.56 us
    ppermute x1, waiting for transfers between devices, body(): other = lax.ppermute(give, 'tmpl', [(0, 1), (1, 0)])  6.1 us
    ppermute x1, starting transfers between devices, body(): other = lax.ppermute(give, 'tmpl', [(0, 1), (1, 0)])  3.7 us
  transfers between devices with their start and end apart: 5, of which 4 were waited for; matrix products, arithmetic and copies ran while one was open for 0% of the time, Pallas kernels for 2%

profile of v4, /device:TPU:1, one launch (start us, length us, event | category | flops | bytes accessed | tf_op | source)
XLA Modules:
  0.0 95.9 jit_solution(18132615521448240844)
XLA Ops:
  0.0 2.6 %shard_map.73 = bf16[64,24,128]{2,1,0:T(8,128)(2,1)} custom-call(bf16[1,32,2048]{2,1,0:T(8,128)(2,1)} %pair.3, bf16[1,32,2048]{2,1,0:T(8,128)(2,1)} %saved.3, bf16[1,32,2048]{2,1,0:T(8,128)(2,1)} %upstream.3, f32[1,64]{1,0:T(1,128)} %bitcast.4, f32[1,64]{1,0:T(1,128)} %bitcast.7, bf16[64,320]{1,0:T(8,128)(2,1)} %w_in.3, bf16[64,64]{1,0:T(8,128)(2,1)} %w_out.1), custom_call_target="tpu_custom_call" | custom-call | flops 100000000 | bytes 1000000 | tf_op jit(solution)/shard_map/pallas_call | solution.py:261
  2.6 28.9 %all_to_all.10.got = bf16[64,24,128]{2,1,0:T(8,128)(2,1)S(1)} all-to-all(bf16[64,24,128]{2,1,0:T(8,128)(2,1)} %shard_map.73), channel_id=1, replica_groups={{0,1,2,3,16,17,18,19,32,33,34,35,48,49,50,51,64,65,66,67,80,81,82,83,96..., dimensions={0} | all-to-all | bytes 786432 | tf_op jit(solution)/shard_map/all_to_all | solution.py:310
  31.5 0.0 copy-start
  31.5 0.0 copy-start.1
  31.5 0.0 copy-start.2
  31.5 0.2 shard_map.75.d0
  31.7 9.8 %collective-permute-start.2 = (bf16[128,512]{1,0:T(8,128)(2,1)S(1)}, bf16[128,512]{1,0:T(8,128)(2,1)S(1)}, u32[]{:S(2)}, u32[]{:S(2)}) collective-permute-start(bf16[128,512]{1,0:T(8,128)(2,1)S(1)} %shard_map.75.d0), channel_id=1, source_target_pairs={{0,12},{1,13},{2,14},{3,15},{4,8},{5,9},{6,10},{7,11},{8,4},{9,5},... | collective-permute-start | bytes 393224 | tf_op jit(solution)/shard_map/ppermute | solution.py:322
  41.5 6.1 %collective-permute-start.1 = (bf16[128,512]{1,0:T(8,128)(2,1)S(1)}, bf16[128,512]{1,0:T(8,128)(2,1)S(1)}, u32[]{:S(2)}, u32[]{:S(2)}) collective-permute-start(bf16[128,512]{1,0:T(8,128)(2,1)S(1)} %shard_map.75.d0), channel_id=1, source_target_pairs={{0,8},{1,9},{2,10},{3,11},{4,12},{5,13},{6,14},{7,15},{8,0},{9,1},... | collective-permute-start | bytes 393224 | tf_op jit(solution)/shard_map/ppermute | solution.py:322
  47.5 2.9 %collective-permute-start = (bf16[128,512]{1,0:T(8,128)(2,1)S(1)}, bf16[128,512]{1,0:T(8,128)(2,1)S(1)}, u32[]{:S(2)}, u32[]{:S(2)}) collective-permute-start(bf16[128,512]{1,0:T(8,128)(2,1)S(1)} %shard_map.75.d0), channel_id=1, source_target_pairs={{0,4},{1,5},{2,6},{3,7},{4,0},{5,1},{6,2},{7,3},{8,12},{9,13},{10,... | collective-permute-start | bytes 393224 | tf_op jit(solution)/shard_map/ppermute | solution.py:322
  50.4 0.0 copy-done
  50.4 0.0 copy-done.1
  50.4 0.0 copy-done.2
  50.5 0.8 shard_map.74
  51.2 10.6 %collective-permute-done.2.d3 = bf16[128,512]{1,0:T(8,128)(2,1)S(1)} collective-permute-done((bf16[128,512]{1,0:T(8,128)(2,1)S(1)}, bf16[128,512]{1,0:T(8,128)(2,1)S(1)}, u32[]{:S(2)}, u32[]{:S(2)}) %collective-permute-start.2) | collective-permute-done | bytes 131104 | tf_op jit(solution)/shard_map/ppermute | solution.py:322
  61.8 9.5 %collective-permute-done.1.d2 = bf16[128,512]{1,0:T(8,128)(2,1)S(1)} collective-permute-done((bf16[128,512]{1,0:T(8,128)(2,1)S(1)}, bf16[128,512]{1,0:T(8,128)(2,1)S(1)}, u32[]{:S(2)}, u32[]{:S(2)}) %collective-permute-start.1) | collective-permute-done | bytes 131104 | tf_op jit(solution)/shard_map/ppermute | solution.py:322
  71.3 0.0 collective-permute-done.d1
  71.3 1.5 %shard_map.76 = bf16[128,8,128]{2,1,0:T(8,128)(2,1)} custom-call(s32[1]{0:T(128)} %bitcast.1.quad_ref, bf16[128,512]{1,0:T(8,128)(2,1)S(1)} %get-tuple-element.12.left_all, bf16[128,512]{1,0:T(8,128)(2,1)S(1)} %get-tuple-element.13.right_all, bf16[128,512]{1,0:T(8,128)(2,1)S(1)} %shard_map.75.d0, bf16[128,512]{1,0:T(8,128)(2,1)S(1)} %collective-permute-done.d1, ...), custom_call_target="tpu_custom_call" | custom-call | flops 100000000 | bytes 1000000 | tf_op jit(solution)/shard_map/pallas_call | solution.py:261
  72.7 0.0 copy-start.3
  72.7 0.0 copy-start.4
  72.7 8.8 %all-to-all-start.1 = ((bf16[128,8,128]{2,1,0:T(8,128)(2,1)}), bf16[128,8,128]{2,1,0:T(8,128)(2,1)S(1)}, u32[]{:S(2)}, u32[]{:S(2)}) async-start(bf16[128,8,128]{2,1,0:T(8,128)(2,1)} %shard_map.76), calls=%async_computation.1 | async-start | bytes 524288 | tf_op jit(solution)/shard_map/all_to_all | solution.py:354
  81.6 0.0 copy-start.5
  81.6 0.0 copy-start.6
  81.6 3.7 %collective-permute-start.3 = (bf16[3,16,2048]{2,1,0:T(8,128)(2,1)S(1)}, bf16[3,16,2048]{2,1,0:T(8,128)(2,1)S(1)}, u32[]{:S(2)}, u32[]{:S(2)}) collective-permute-start(bf16[3,16,2048]{2,1,0:T(8,128)(2,1)S(1)} %get-tuple-element.14), channel_id=1, source_target_pairs={{0,256},{256,0},{1,257},{257,1},{2,258},{258,2},{3,259},{259,3},{4... | collective-permute-start | bytes 589832 | tf_op jit(solution)/shard_map/ppermute | solution.py:319
  85.3 6.1 %collective-permute-done.3.other = bf16[3,16,2048]{2,1,0:T(8,128)(2,1)S(1)} collective-permute-done((bf16[3,16,2048]{2,1,0:T(8,128)(2,1)S(1)}, bf16[3,16,2048]{2,1,0:T(8,128)(2,1)S(1)}, u32[]{:S(2)}, u32[]{:S(2)}) %collective-permute-start.3) | collective-permute-done | bytes 196640 | tf_op jit(solution)/shard_map/ppermute | solution.py:319
  91.4 0.0 copy-done.3
  91.4 0.0 copy-done.4
  91.4 0.0 copy-done.5
  91.4 0.0 copy-done.6
  91.4 1.2 %shard_map.77 = (f32[4,64,1024]{2,1,0:T(8,128)S(1)}, f32[64,1024]{1,0:T(8,128)S(1)}, f32[64,1024]{1,0:T(8,128)S(1)}, f32[1,1024]{1,0:T(1,128)S(1)}) custom-call(s32[1]{0:T(128)} %bitcast.mine_ref, bf16[1,32,2048]{2,1,0:T(8,128)(2,1)S(1)} %copy-done, bf16[1,32,2048]{2,1,0:T(8,128)(2,1)S(1)} %copy-done.1, bf16[1,32,2048]{2,1,0:T(8,128)(2,1)S(1)} %copy-done.2, ...), custom_call_target="tpu_custom_call" | custom-call | flops 100000000 | bytes 1000000 | tf_op jit(solution)/shard_map/pallas_call | solution.py:261
  92.7 1.9 %all-to-all-done.1.home = bf16[128,8,128]{2,1,0:T(8,128)(2,1)S(1)} async-done(((bf16[128,8,128]{2,1,0:T(8,128)(2,1)}), bf16[128,8,128]{2,1,0:T(8,128)(2,1)S(1)}, u32[]{:S(2)}, u32[]{:S(2)}) %all-to-all-start.1) | async-done | bytes 262176 | tf_op jit(solution)/shard_map/all_to_all | solution.py:354
  94.6 1.3 %shard_map.78 = f32[16,2048]{1,0:T(8,128)} custom-call(s32[1]{0:T(128)} %bitcast.mine_ref, bf16[128,8,128]{2,1,0:T(8,128)(2,1)S(1)} %all-to-all-done.1.home, f32[4,64,1024]{2,1,0:T(8,128)S(1)} %get-tuple-element.15.factors, f32[64,1024]{1,0:T(8,128)S(1)} %get-tuple-element.16.rest, f32[64,1024]{1,0:T(8,128)S(1)} %get-tuple-element.17.units, ...), custom_call_target="tpu_custom_call" | custom-call | flops 100000000 | bytes 1000000 | tf_op jit(solution)/shard_map/pallas_call | solution.py:261
Async XLA Ops:
  31.5 18.9 %copy-start = (bf16[1,32,2048]{2,1,0:T(8,128)(2,1)S(1)}, bf16[1,32,2048]{2,1,0:T(8,128)(2,1)}, u32[]{:S(2)}) copy-start(bf16[1,32,2048]{2,1,0:T(8,128)(2,1)} %pair.3) | copy-start | bytes 393220
  31.5 18.9 %copy-start.1 = (bf16[1,32,2048]{2,1,0:T(8,128)(2,1)S(1)}, bf16[1,32,2048]{2,1,0:T(8,128)(2,1)}, u32[]{:S(2)}) copy-start(bf16[1,32,2048]{2,1,0:T(8,128)(2,1)} %saved.3) | copy-start | bytes 393220
  31.5 18.9 %copy-start.2 = (bf16[1,32,2048]{2,1,0:T(8,128)(2,1)S(1)}, bf16[1,32,2048]{2,1,0:T(8,128)(2,1)}, u32[]{:S(2)}) copy-start(bf16[1,32,2048]{2,1,0:T(8,128)(2,1)} %upstream.3) | copy-start | bytes 393220
  31.7 30.1 %collective-permute-start.2 = (bf16[128,512]{1,0:T(8,128)(2,1)S(1)}, bf16[128,512]{1,0:T(8,128)(2,1)S(1)}, u32[]{:S(2)}, u32[]{:S(2)}) collective-permute-start(bf16[128,512]{1,0:T(8,128)(2,1)S(1)} %shard_map.75.d0), channel_id=1, source_target_pairs={{0,12},{1,13},{2,14},{3,15},{4,8},{5,9},{6,10},{7,11},{8,4},{9,5},... | collective-permute-start | bytes 393224 | tf_op jit(solution)/shard_map/ppermute | solution.py:322
  41.5 29.8 %collective-permute-start.1 = (bf16[128,512]{1,0:T(8,128)(2,1)S(1)}, bf16[128,512]{1,0:T(8,128)(2,1)S(1)}, u32[]{:S(2)}, u32[]{:S(2)}) collective-permute-start(bf16[128,512]{1,0:T(8,128)(2,1)S(1)} %shard_map.75.d0), channel_id=1, source_target_pairs={{0,8},{1,9},{2,10},{3,11},{4,12},{5,13},{6,14},{7,15},{8,0},{9,1},... | collective-permute-start | bytes 393224 | tf_op jit(solution)/shard_map/ppermute | solution.py:322
  47.5 23.7 %collective-permute-start = (bf16[128,512]{1,0:T(8,128)(2,1)S(1)}, bf16[128,512]{1,0:T(8,128)(2,1)S(1)}, u32[]{:S(2)}, u32[]{:S(2)}) collective-permute-start(bf16[128,512]{1,0:T(8,128)(2,1)S(1)} %shard_map.75.d0), channel_id=1, source_target_pairs={{0,4},{1,5},{2,6},{3,7},{4,0},{5,1},{6,2},{7,3},{8,12},{9,13},{10,... | collective-permute-start | bytes 393224 | tf_op jit(solution)/shard_map/ppermute | solution.py:322
  72.7 18.7 %copy-start.3 = (bf16[64,320]{1,0:T(8,128)(2,1)S(1)}, bf16[64,320]{1,0:T(8,128)(2,1)}, u32[]{:S(2)}) copy-start(bf16[64,320]{1,0:T(8,128)(2,1)} %w_in.3) | copy-start | bytes 122884
  72.7 18.7 %copy-start.4 = (bf16[64,64]{1,0:T(8,128)(2,1)S(1)}, bf16[64,64]{1,0:T(8,128)(2,1)}, u32[]{:S(2)}) copy-start(bf16[64,64]{1,0:T(8,128)(2,1)} %w_out.1) | copy-start | bytes 24580
  72.7 21.9 %all-to-all-start.1 = ((bf16[128,8,128]{2,1,0:T(8,128)(2,1)}), bf16[128,8,128]{2,1,0:T(8,128)(2,1)S(1)}, u32[]{:S(2)}, u32[]{:S(2)}) async-start(bf16[128,8,128]{2,1,0:T(8,128)(2,1)} %shard_map.76), calls=%async_computation.1 | async-start | bytes 524288 | tf_op jit(solution)/shard_map/all_to_all | solution.py:354
  81.6 9.8 %copy-start.5 = (f32[64]{0:T(128)S(1)}, f32[64]{0:T(128)}, u32[]{:S(2)}) copy-start(f32[64]{0:T(128)} %param.10) | copy-start | bytes 772
  81.6 9.8 %copy-start.6 = (f32[64]{0:T(128)S(1)}, f32[64]{0:T(128)}, u32[]{:S(2)}) copy-start(f32[64]{0:T(128)} %param.11) | copy-start | bytes 772
  81.6 9.8 %collective-permute-start.3 = (bf16[3,16,2048]{2,1,0:T(8,128)(2,1)S(1)}, bf16[3,16,2048]{2,1,0:T(8,128)(2,1)S(1)}, u32[]{:S(2)}, u32[]{:S(2)}) collective-permute-start(bf16[3,16,2048]{2,1,0:T(8,128)(2,1)S(1)} %get-tuple-element.14), channel_id=1, source_target_pairs={{0,256},{256,0},{1,257},{257,1},{2,258},{258,2},{3,259},{259,3},{4... | collective-permute-start | bytes 589832 | tf_op jit(solution)/shard_map/ppermute | solution.py:319

commit v5 on v4

--- a/solution.py
+++ b/solution.py
@@ -1,3 +1,5 @@
+import functools
+
 import jax
 import jax.numpy as jnp
 from jax import lax
@@ -143,9 +145,9 @@
         out[row : row + 16, columns] = value
 
 
-def operand_kernel(mine_ref, got, pair, saved, upstream, left_all, right_all, give):
+def operand_kernel(got, pair, saved, upstream, left_all, right_all, give):
     lane = lanes_of(8)
-    first = pl.multiple_of((1 - mine_ref[0]) * 16, 16)
+    first = pl.multiple_of((1 - lax.axis_index("tmpl")) * 16, 16)
     for n, ref in enumerate((pair, saved, upstream)):
         give[n] = ref[0, pl.ds(first, 16), :]
     for n, out in ((1, left_all), (2, right_all)):
@@ -153,8 +155,8 @@
             out[row : row + 16, columns] = value
 
 
-def product_kernel(quad_ref, left_all, right_all, d0, d1, d2, d3, back, d_left, d_right):
-    quad = quad_ref[0]
+def product_kernel(near, left_all, right_all, d0, d1, d2, d3, back, d_left, d_right):
+    quad = lax.axis_index("col") // near
     total = None
     left = left_all[...]
     for s, d_ref in enumerate((d0, d1, d2, d3)):
@@ -181,19 +183,20 @@
                 back[half * 64 + r * 4 + m] = chunk.astype(BF16)
 
 
-def prepare_kernel(mine_ref, pair, saved, upstream, other, in_gain, out_gain, w_in, w_out, factors, rest, units, invs):
+def prepare_kernel(pair, saved, upstream, other, in_gain, out_gain, w_in, w_out, factors, rest, units, invs):
     channels = w_out.shape[0]
-    first = pl.multiple_of(mine_ref[0] * 16, 16)
+    mine = lax.axis_index("tmpl")
+    first = pl.multiple_of(mine * 16, 16)
     gain_in, gain_out = column(in_gain), column(out_gain)
     weights, weights_out = w_in[...], w_out[...]
     for b in range(4):
 
         def tile(n, ref):
             spans = [slice((4 * k + b) * LANES, (4 * k + b + 1) * LANES) for k in range(4)]
-            return turn(
-                [ref[0, pl.ds(first, 16), span] for span in spans]
-                + [other[n, :, span] for span in spans]
-            )
+            here = jnp.concatenate([ref[0, pl.ds(first, 16), span] for span in spans], axis=0)
+            there = jnp.concatenate([other[n, :, span] for span in spans], axis=0)
+            here, there = here.astype(F32), there.astype(F32)
+            return turn([jnp.where(mine == 0, here, there), jnp.where(mine == 0, there, here)])
 
         span = slice(2 * b * LANES, (2 * b + 2) * LANES)
         normed, unit, inv = normalize(tile(0, pair), gain_in)
@@ -211,16 +214,14 @@
         rest[:, span] = dot(weights[:, 4 * channels :], d_og, ((1,), (0,)))
 
 
-def finish_kernel(mine_ref, home, factors, rest, units, invs, in_gain, w_in, out, held):
+def finish_kernel(home, factors, rest, units, invs, in_gain, w_in, out, held):
     channels = rest.shape[0]
-    mine = mine_ref[0]
     gain_in = column(in_gain)
     weights = w_in[:, : 4 * channels]
     for t in range(2):
-        base = lax.rem(mine + t, 2) * channels
         for c in range(channels):
             at = (t * channels + c) * 8
-            held[at : at + 8, :] = home[base + c].astype(F32)
+            held[at : at + 8, :] = home[t * channels + c].astype(F32)
     low = lanes_of(channels) < LANES // 2
     d_lefts, d_rights = [], []
     for g in range(8):
@@ -253,15 +254,14 @@
 
 
 VMEM = pl.BlockSpec(memory_space=pltpu.VMEM)
-SMEM = pl.BlockSpec(memory_space=pltpu.SMEM)
 HBM = pl.BlockSpec(memory_space=pltpu.HBM)
 
 
-def call(kernel, outs, args, scratch=(), scalars=0, cost=1, limit=16, space=VMEM, out_space=VMEM):
+def call(kernel, outs, args, scratch=(), cost=1, limit=16, space=VMEM, out_space=VMEM):
     return pl.pallas_call(
         kernel,
         out_shape=outs,
-        in_specs=[SMEM] * scalars + [space] * (len(args) - scalars),
+        in_specs=[space] * len(args),
         out_specs=jax.tree.map(lambda _: out_space, outs),
         scratch_shapes=list(scratch),
         compiler_params=pltpu.CompilerParams(vmem_limit_bytes=limit * 2**20),
@@ -281,9 +281,6 @@
         _, tile_rows, merged = pair.shape
         half = tile_rows // tmpl_n
         in_gain, out_gain = in_gain[None], out_gain[None]
-        mine = lax.axis_index("tmpl")
-        quad = lax.axis_index("col") // near
-        mine1, quad1 = mine[None].astype(jnp.int32), quad[None].astype(jnp.int32)
         cells = tile_rows * merged // channels
         count = cells // LANES
 
@@ -311,10 +308,9 @@
         panel = shaped((LANES, rows_n * tile_rows), BF16)
         d_own = call(cotangent_kernel, panel, (got,))
         left_all, right_all, give = call(
-            operand_kernel,
-            (panel, panel, shaped((3, half, merged), BF16)),
-            (mine1, got, pair, saved, upstream),
-            scalars=1,
+        operand_kernel,
+        (panel, panel, shaped((3, half, merged), BF16)),
+        (got, pair, saved, upstream),
         )
         other = lax.ppermute(give, "tmpl", [(0, 1), (1, 0)])
         far = {}
@@ -324,23 +320,21 @@
             )
 
         factors, rest, units, invs = call(
-            prepare_kernel,
-            (
-                shaped((4, channels, cells), F32),
-                shaped((channels, cells), F32),
-                shaped((channels, cells), F32),
-                shaped((1, cells), F32),
-            ),
-            (mine1, pair, saved, upstream, other, in_gain, out_gain, w_in, w_out),
-            scalars=1,
+        prepare_kernel,
+        (
+            shaped((4, channels, cells), F32),
+            shaped((channels, cells), F32),
+            shaped((channels, cells), F32),
+            shaped((1, cells), F32),
+        ),
+        (pair, saved, upstream, other, in_gain, out_gain, w_in, w_out),
         )
 
         back = call(
-            product_kernel,
+            functools.partial(product_kernel, near),
             shaped((tmpl_n * channels, count, LANES), BF16),
-            (quad1, left_all, right_all, d_own, far[1], far[2], far[3]),
+            (left_all, right_all, d_own, far[1], far[2], far[3]),
             scratch=[pltpu.VMEM((LANES, rows_n * tile_rows), F32)] * 2,
-            scalars=1,
         )
         groups = [
             [
@@ -357,9 +351,8 @@
         return call(
             finish_kernel,
             shaped((half, merged), F32),
-            (mine1, home, factors, rest, units, invs, in_gain, w_in),
+            (home, factors, rest, units, invs, in_gain, w_in),
             scratch=[pltpu.VMEM((tmpl_n * channels * count, LANES), F32)],
-            scalars=1,
         )
 
     in_specs = (P("tmpl", "row", "col"),) * 3 + (P(),) * 4

time: 96.3 us -> 96.3 us (level)
  no operation moved by 1% of the time
where the time goes in v5:
time: 96.3 us; the launch traced here: 95.9 us
  starting transfers between devices  31.2 us (32%)
  blocking collectives  28.9 us (30%)
  waiting for transfers between devices  28.1 us (29%)
  Pallas kernels  7.58 us (8%)
    all_to_all x1, blocking collectives, body(): lax.all_to_all(send, ('row', 'col'), 0, 0, axis_index_groups=groups, tile...  28.9 us
    ppermute x3, waiting for transfers between devices, body(): lax.ppermute(d_own, 'col', [(z, z ^ near * s) for z in range(cols_n)])  20.1 us
    ppermute x3, starting transfers between devices, body(): lax.ppermute(d_own, 'col', [(z, z ^ near * s) for z in range(cols_n)])  18.7 us
    all_to_all x1, starting transfers between devices, body(): lax.all_to_all(back, ('tmpl', 'row', 'col'), 0, 0, axis_index_groups=grou...  8.83 us
    pallas_call x6, Pallas kernels, call(): pl.pallas_call(kernel, out_shape=outs, in_specs=[space] * len(args), out_...  7.58 us
    ppermute x1, waiting for transfers between devices, body(): other = lax.ppermute(give, 'tmpl', [(0, 1), (1, 0)])  6.1 us
    ppermute x1, starting transfers between devices, body(): other = lax.ppermute(give, 'tmpl', [(0, 1), (1, 0)])  3.7 us
  transfers between devices with their start and end apart: 5, of which 4 were waited for; matrix products, arithmetic and copies ran while one was open for 0% of the time, Pallas kernels for 2%

profile of v5, /device:TPU:1, one launch (start us, length us, event | category | flops | bytes accessed | tf_op | source)
XLA Modules:
  0.0 95.9 jit_solution(11748015434862094216)
XLA Ops:
  0.0 2.6 %shard_map.73 = bf16[64,24,128]{2,1,0:T(8,128)(2,1)} custom-call(bf16[1,32,2048]{2,1,0:T(8,128)(2,1)} %pair.3, bf16[1,32,2048]{2,1,0:T(8,128)(2,1)} %saved.3, bf16[1,32,2048]{2,1,0:T(8,128)(2,1)} %upstream.3, f32[1,64]{1,0:T(1,128)} %bitcast.2, f32[1,64]{1,0:T(1,128)} %bitcast.5, bf16[64,320]{1,0:T(8,128)(2,1)} %w_in.3, bf16[64,64]{1,0:T(8,128)(2,1)} %w_out.1), custom_call_target="tpu_custom_call" | custom-call | flops 100000000 | bytes 1000000 | tf_op jit(solution)/shard_map/pallas_call | solution.py:261
  2.6 28.9 %all_to_all.10.got = bf16[64,24,128]{2,1,0:T(8,128)(2,1)S(1)} all-to-all(bf16[64,24,128]{2,1,0:T(8,128)(2,1)} %shard_map.73), channel_id=1, replica_groups={{0,1,2,3,16,17,18,19,32,33,34,35,48,49,50,51,64,65,66,67,80,81,82,83,96..., dimensions={0} | all-to-all | bytes 786432 | tf_op jit(solution)/shard_map/all_to_all | solution.py:307
  31.5 0.0 copy-start
  31.5 0.0 copy-start.1
  31.5 0.0 copy-start.2
  31.5 0.2 shard_map.75.d0
  31.7 9.8 %collective-permute-start.2 = (bf16[128,512]{1,0:T(8,128)(2,1)S(1)}, bf16[128,512]{1,0:T(8,128)(2,1)S(1)}, u32[]{:S(2)}, u32[]{:S(2)}) collective-permute-start(bf16[128,512]{1,0:T(8,128)(2,1)S(1)} %shard_map.75.d0), channel_id=1, source_target_pairs={{0,12},{1,13},{2,14},{3,15},{4,8},{5,9},{6,10},{7,11},{8,4},{9,5},... | collective-permute-start | bytes 393224 | tf_op jit(solution)/shard_map/ppermute | solution.py:318
  41.5 6.1 %collective-permute-start.1 = (bf16[128,512]{1,0:T(8,128)(2,1)S(1)}, bf16[128,512]{1,0:T(8,128)(2,1)S(1)}, u32[]{:S(2)}, u32[]{:S(2)}) collective-permute-start(bf16[128,512]{1,0:T(8,128)(2,1)S(1)} %shard_map.75.d0), channel_id=1, source_target_pairs={{0,8},{1,9},{2,10},{3,11},{4,12},{5,13},{6,14},{7,15},{8,0},{9,1},... | collective-permute-start | bytes 393224 | tf_op jit(solution)/shard_map/ppermute | solution.py:318
  47.5 2.9 %collective-permute-start = (bf16[128,512]{1,0:T(8,128)(2,1)S(1)}, bf16[128,512]{1,0:T(8,128)(2,1)S(1)}, u32[]{:S(2)}, u32[]{:S(2)}) collective-permute-start(bf16[128,512]{1,0:T(8,128)(2,1)S(1)} %shard_map.75.d0), channel_id=1, source_target_pairs={{0,4},{1,5},{2,6},{3,7},{4,0},{5,1},{6,2},{7,3},{8,12},{9,13},{10,... | collective-permute-start | bytes 393224 | tf_op jit(solution)/shard_map/ppermute | solution.py:318
  50.4 0.0 copy-done
  50.4 0.0 copy-done.1
  50.4 0.0 copy-done.2
  50.4 0.8 shard_map.74
  51.2 10.6 %collective-permute-done.2.d3 = bf16[128,512]{1,0:T(8,128)(2,1)S(1)} collective-permute-done((bf16[128,512]{1,0:T(8,128)(2,1)S(1)}, bf16[128,512]{1,0:T(8,128)(2,1)S(1)}, u32[]{:S(2)}, u32[]{:S(2)}) %collective-permute-start.2) | collective-permute-done | bytes 131104 | tf_op jit(solution)/shard_map/ppermute | solution.py:318
  61.8 9.5 %collective-permute-done.1.d2 = bf16[128,512]{1,0:T(8,128)(2,1)S(1)} collective-permute-done((bf16[128,512]{1,0:T(8,128)(2,1)S(1)}, bf16[128,512]{1,0:T(8,128)(2,1)S(1)}, u32[]{:S(2)}, u32[]{:S(2)}) %collective-permute-start.1) | collective-permute-done | bytes 131104 | tf_op jit(solution)/shard_map/ppermute | solution.py:318
  71.3 0.0 collective-permute-done.d1
  71.3 1.4 %shard_map.76 = bf16[128,8,128]{2,1,0:T(8,128)(2,1)} custom-call(bf16[128,512]{1,0:T(8,128)(2,1)S(1)} %get-tuple-element.12.left_all, bf16[128,512]{1,0:T(8,128)(2,1)S(1)} %get-tuple-element.13.right_all, bf16[128,512]{1,0:T(8,128)(2,1)S(1)} %shard_map.75.d0, bf16[128,512]{1,0:T(8,128)(2,1)S(1)} %collective-permute-done.d1, ...), custom_call_target="tpu_custom_call" | custom-call | flops 100000000 | bytes 1000000 | tf_op jit(solution)/shard_map/pallas_call | solution.py:261
  72.7 0.0 copy-start.3
  72.7 0.0 copy-start.4
  72.7 8.8 %all-to-all-start.1 = ((bf16[128,8,128]{2,1,0:T(8,128)(2,1)}), bf16[128,8,128]{2,1,0:T(8,128)(2,1)S(1)}, u32[]{:S(2)}, u32[]{:S(2)}) async-start(bf16[128,8,128]{2,1,0:T(8,128)(2,1)} %shard_map.76), calls=%async_computation.1 | async-start | bytes 524288 | tf_op jit(solution)/shard_map/all_to_all | solution.py:348
  81.6 0.0 copy-start.5
  81.6 0.0 copy-start.6
  81.6 3.7 %collective-permute-start.3 = (bf16[3,16,2048]{2,1,0:T(8,128)(2,1)S(1)}, bf16[3,16,2048]{2,1,0:T(8,128)(2,1)S(1)}, u32[]{:S(2)}, u32[]{:S(2)}) collective-permute-start(bf16[3,16,2048]{2,1,0:T(8,128)(2,1)S(1)} %get-tuple-element.14), channel_id=1, source_target_pairs={{0,256},{256,0},{1,257},{257,1},{2,258},{258,2},{3,259},{259,3},{4... | collective-permute-start | bytes 589832 | tf_op jit(solution)/shard_map/ppermute | solution.py:315
  85.3 6.1 %collective-permute-done.3.other = bf16[3,16,2048]{2,1,0:T(8,128)(2,1)S(1)} collective-permute-done((bf16[3,16,2048]{2,1,0:T(8,128)(2,1)S(1)}, bf16[3,16,2048]{2,1,0:T(8,128)(2,1)S(1)}, u32[]{:S(2)}, u32[]{:S(2)}) %collective-permute-start.3) | collective-permute-done | bytes 196640 | tf_op jit(solution)/shard_map/ppermute | solution.py:315
  91.4 0.0 copy-done.3
  91.4 0.0 copy-done.4
  91.4 0.0 copy-done.5
  91.4 0.0 copy-done.6
  91.4 1.2 %shard_map.77 = (f32[4,64,1024]{2,1,0:T(8,128)S(1)}, f32[64,1024]{1,0:T(8,128)S(1)}, f32[64,1024]{1,0:T(8,128)S(1)}, f32[1,1024]{1,0:T(1,128)S(1)}) custom-call(bf16[1,32,2048]{2,1,0:T(8,128)(2,1)S(1)} %copy-done, bf16[1,32,2048]{2,1,0:T(8,128)(2,1)S(1)} %copy-done.1, bf16[1,32,2048]{2,1,0:T(8,128)(2,1)S(1)} %copy-done.2, ...), custom_call_target="tpu_custom_call" | custom-call | flops 100000000 | bytes 1000000 | tf_op jit(solution)/shard_map/pallas_call | solution.py:261
  92.7 1.9 %all-to-all-done.1.home = bf16[128,8,128]{2,1,0:T(8,128)(2,1)S(1)} async-done(((bf16[128,8,128]{2,1,0:T(8,128)(2,1)}), bf16[128,8,128]{2,1,0:T(8,128)(2,1)S(1)}, u32[]{:S(2)}, u32[]{:S(2)}) %all-to-all-start.1) | async-done | bytes 262176 | tf_op jit(solution)/shard_map/all_to_all | solution.py:348
  94.6 1.3 %shard_map.78 = f32[16,2048]{1,0:T(8,128)} custom-call(bf16[128,8,128]{2,1,0:T(8,128)(2,1)S(1)} %all-to-all-done.1.home, f32[4,64,1024]{2,1,0:T(8,128)S(1)} %get-tuple-element.15.factors, f32[64,1024]{1,0:T(8,128)S(1)} %get-tuple-element.16.rest, f32[64,1024]{1,0:T(8,128)S(1)} %get-tuple-element.17.units, f32[1,1024]{1,0:T(1,128)S(1)} %get-tuple-element.18.invs, ...), custom_call_target="tpu_custom_call" | custom-call | flops 100000000 | bytes 1000000 | tf_op jit(solution)/shard_map/pallas_call | solution.py:261
Async XLA Ops:
  31.5 18.9 %copy-start = (bf16[1,32,2048]{2,1,0:T(8,128)(2,1)S(1)}, bf16[1,32,2048]{2,1,0:T(8,128)(2,1)}, u32[]{:S(2)}) copy-start(bf16[1,32,2048]{2,1,0:T(8,128)(2,1)} %pair.3) | copy-start | bytes 393220
  31.5 18.9 %copy-start.1 = (bf16[1,32,2048]{2,1,0:T(8,128)(2,1)S(1)}, bf16[1,32,2048]{2,1,0:T(8,128)(2,1)}, u32[]{:S(2)}) copy-start(bf16[1,32,2048]{2,1,0:T(8,128)(2,1)} %saved.3) | copy-start | bytes 393220
  31.5 18.9 %copy-start.2 = (bf16[1,32,2048]{2,1,0:T(8,128)(2,1)S(1)}, bf16[1,32,2048]{2,1,0:T(8,128)(2,1)}, u32[]{:S(2)}) copy-start(bf16[1,32,2048]{2,1,0:T(8,128)(2,1)} %upstream.3) | copy-start | bytes 393220
  31.7 30.1 %collective-permute-start.2 = (bf16[128,512]{1,0:T(8,128)(2,1)S(1)}, bf16[128,512]{1,0:T(8,128)(2,1)S(1)}, u32[]{:S(2)}, u32[]{:S(2)}) collective-permute-start(bf16[128,512]{1,0:T(8,128)(2,1)S(1)} %shard_map.75.d0), channel_id=1, source_target_pairs={{0,12},{1,13},{2,14},{3,15},{4,8},{5,9},{6,10},{7,11},{8,4},{9,5},... | collective-permute-start | bytes 393224 | tf_op jit(solution)/shard_map/ppermute | solution.py:318
  41.5 29.8 %collective-permute-start.1 = (bf16[128,512]{1,0:T(8,128)(2,1)S(1)}, bf16[128,512]{1,0:T(8,128)(2,1)S(1)}, u32[]{:S(2)}, u32[]{:S(2)}) collective-permute-start(bf16[128,512]{1,0:T(8,128)(2,1)S(1)} %shard_map.75.d0), channel_id=1, source_target_pairs={{0,8},{1,9},{2,10},{3,11},{4,12},{5,13},{6,14},{7,15},{8,0},{9,1},... | collective-permute-start | bytes 393224 | tf_op jit(solution)/shard_map/ppermute | solution.py:318
  47.5 23.7 %collective-permute-start = (bf16[128,512]{1,0:T(8,128)(2,1)S(1)}, bf16[128,512]{1,0:T(8,128)(2,1)S(1)}, u32[]{:S(2)}, u32[]{:S(2)}) collective-permute-start(bf16[128,512]{1,0:T(8,128)(2,1)S(1)} %shard_map.75.d0), channel_id=1, source_target_pairs={{0,4},{1,5},{2,6},{3,7},{4,0},{5,1},{6,2},{7,3},{8,12},{9,13},{10,... | collective-permute-start | bytes 393224 | tf_op jit(solution)/shard_map/ppermute | solution.py:318
  72.7 18.7 %copy-start.3 = (bf16[64,320]{1,0:T(8,128)(2,1)S(1)}, bf16[64,320]{1,0:T(8,128)(2,1)}, u32[]{:S(2)}) copy-start(bf16[64,320]{1,0:T(8,128)(2,1)} %w_in.3) | copy-start | bytes 122884
  72.7 18.7 %copy-start.4 = (bf16[64,64]{1,0:T(8,128)(2,1)S(1)}, bf16[64,64]{1,0:T(8,128)(2,1)}, u32[]{:S(2)}) copy-start(bf16[64,64]{1,0:T(8,128)(2,1)} %w_out.1) | copy-start | bytes 24580
  72.7 21.9 %all-to-all-start.1 = ((bf16[128,8,128]{2,1,0:T(8,128)(2,1)}), bf16[128,8,128]{2,1,0:T(8,128)(2,1)S(1)}, u32[]{:S(2)}, u32[]{:S(2)}) async-start(bf16[128,8,128]{2,1,0:T(8,128)(2,1)} %shard_map.76), calls=%async_computation.1 | async-start | bytes 524288 | tf_op jit(solution)/shard_map/all_to_all | solution.py:348
  81.6 9.8 %copy-start.5 = (f32[64]{0:T(128)S(1)}, f32[64]{0:T(128)}, u32[]{:S(2)}) copy-start(f32[64]{0:T(128)} %param.10) | copy-start | bytes 772
  81.6 9.8 %copy-start.6 = (f32[64]{0:T(128)S(1)}, f32[64]{0:T(128)}, u32[]{:S(2)}) copy-start(f32[64]{0:T(128)} %param.11) | copy-start | bytes 772
  81.6 9.8 %collective-permute-start.3 = (bf16[3,16,2048]{2,1,0:T(8,128)(2,1)S(1)}, bf16[3,16,2048]{2,1,0:T(8,128)(2,1)S(1)}, u32[]{:S(2)}, u32[]{:S(2)}) collective-permute-start(bf16[3,16,2048]{2,1,0:T(8,128)(2,1)S(1)} %get-tuple-element.14), channel_id=1, source_target_pairs={{0,256},{256,0},{1,257},{257,1},{2,258},{258,2},{3,259},{259,3},{4... | collective-permute-start | bytes 589832 | tf_op jit(solution)/shard_map/ppermute | solution.py:315

commit v6 on v4

--- a/solution.py
+++ b/solution.py
@@ -101,21 +101,28 @@
         span = slice(2 * b * LANES, (2 * b + 2) * LANES)
         proj = dot(weights, normed[:, span], ((0,), (0,)))
         gate = [proj[n * channels : (n + 1) * channels] for n in range(5)]
-        hold(1, 2 * b, jax.nn.sigmoid(gate[0]) * gate[1])
-        hold(2, 2 * b, jax.nn.sigmoid(gate[2]) * gate[3])
+        hold(0, 2 * b, jax.nn.sigmoid(gate[0]) * gate[1])
+        hold(1, 2 * b, jax.nn.sigmoid(gate[2]) * gate[3])
         mixed.append((up[:, span] * jax.nn.sigmoid(gate[4])).astype(BF16))
+    leaves = []
+
+    def leave_with(part, panels):
+        for c in range(channels // 8):
+            for u in range(8):
+                for n in panels:
+                    staged[8 * c + u, 8 * n : 8 * n + 8] = held[
+                        pl.ds((c * 3 + n) * 64 + u, 8, stride=8), :
+                    ].astype(BF16)
+        block = pl.ds(8 * panels[0], 8 * len(panels))
+        leaves.append(
+            pltpu.make_async_copy(staged.at[:, block], send.at[:, block], sent.at[part])
+        )
+        leaves[-1].start()
+
+    leave_with(0, (0, 1))
     d_norm = dot(weights_out, jnp.concatenate(mixed, axis=1), ((1,), (0,)))
-    hold(0, 0, norm_back(d_norm, unit, inv, gain_out))
-    leaves = []
-    for c in range(channels // 8):
-        for u in range(8):
-            for n in range(3):
-                staged[8 * c + u, 8 * n : 8 * n + 8] = held[
-                    pl.ds((c * 3 + n) * 64 + u, 8, stride=8), :
-                ].astype(BF16)
-        rows = pl.ds(8 * c, 8)
-        leaves.append(pltpu.make_async_copy(staged.at[rows], send.at[rows], sent.at[c]))
-        leaves[-1].start()
+    hold(2, 0, norm_back(d_norm, unit, inv, gain_out))
+    leave_with(1, (2,))
     for leave in leaves:
         leave.wait()
 
@@ -139,7 +146,7 @@
 
 
 def cotangent_kernel(got, out):
-    for row, columns, value in collect(got, 0, lanes_of(8)):
+    for row, columns, value in collect(got, 2, lanes_of(8)):
         out[row : row + 16, columns] = value
 
 
@@ -148,7 +155,7 @@
     first = pl.multiple_of((1 - mine_ref[0]) * 16, 16)
     for n, ref in enumerate((pair, saved, upstream)):
         give[n] = ref[0, pl.ds(first, 16), :]
-    for n, out in ((1, left_all), (2, right_all)):
+    for n, out in ((0, left_all), (1, right_all)):
         for row, columns, value in collect(got, n, lane):
             out[row : row + 16, columns] = value
 

time: 96.3 us -> 96.3 us (level)
  no operation moved by 1% of the time
where the time goes in v6:
time: 96.3 us; the launch traced here: 95.9 us
  starting transfers between devices  31.2 us (32%)
  blocking collectives  28.9 us (30%)
  waiting for transfers between devices  28.1 us (29%)
  Pallas kernels  7.55 us (8%)
    all_to_all x1, blocking collectives, body(): lax.all_to_all(send, ('row', 'col'), 0, 0, axis_index_groups=groups, tile...  28.9 us
    ppermute x3, waiting for transfers between devices, body(): lax.ppermute(d_own, 'col', [(z, z ^ near * s) for z in range(cols_n)])  20 us
    ppermute x3, starting transfers between devices, body(): lax.ppermute(d_own, 'col', [(z, z ^ near * s) for z in range(cols_n)])  18.7 us
    all_to_all x1, starting transfers between devices, body(): lax.all_to_all(back, ('tmpl', 'row', 'col'), 0, 0, axis_index_groups=grou...  8.83 us
    pallas_call x6, Pallas kernels, call(): pl.pallas_call(kernel, out_shape=outs, in_specs=[SMEM] * scalars + [space...  7.55 us
    ppermute x1, waiting for transfers between devices, body(): other = lax.ppermute(give, 'tmpl', [(0, 1), (1, 0)])  6.1 us
    ppermute x1, starting transfers between devices, body(): other = lax.ppermute(give, 'tmpl', [(0, 1), (1, 0)])  3.7 us
  transfers between devices with their start and end apart: 5, of which 4 were waited for; matrix products, arithmetic and copies ran while one was open for 0% of the time, Pallas kernels for 2%

profile of v6, /device:TPU:1, one launch (start us, length us, event | category | flops | bytes accessed | tf_op | source)
XLA Modules:
  0.0 95.9 jit_solution(16824732244783606742)
XLA Ops:
  0.0 2.6 %shard_map.73 = bf16[64,24,128]{2,1,0:T(8,128)(2,1)} custom-call(bf16[1,32,2048]{2,1,0:T(8,128)(2,1)} %pair.3, bf16[1,32,2048]{2,1,0:T(8,128)(2,1)} %saved.3, bf16[1,32,2048]{2,1,0:T(8,128)(2,1)} %upstream.3, f32[1,64]{1,0:T(1,128)} %bitcast.4, f32[1,64]{1,0:T(1,128)} %bitcast.7, bf16[64,320]{1,0:T(8,128)(2,1)} %w_in.3, bf16[64,64]{1,0:T(8,128)(2,1)} %w_out.1), custom_call_target="tpu_custom_call" | custom-call | flops 100000000 | bytes 1000000 | tf_op jit(solution)/shard_map/pallas_call | solution.py:268
  2.6 28.9 %all_to_all.10.got = bf16[64,24,128]{2,1,0:T(8,128)(2,1)S(1)} all-to-all(bf16[64,24,128]{2,1,0:T(8,128)(2,1)} %shard_map.73), channel_id=1, replica_groups={{0,1,2,3,16,17,18,19,32,33,34,35,48,49,50,51,64,65,66,67,80,81,82,83,96..., dimensions={0} | all-to-all | bytes 786432 | tf_op jit(solution)/shard_map/all_to_all | solution.py:317
  31.5 0.0 copy-start
  31.5 0.0 copy-start.1
  31.5 0.0 copy-start.2
  31.5 0.2 shard_map.75.d0
  31.7 9.8 %collective-permute-start.2 = (bf16[128,512]{1,0:T(8,128)(2,1)S(1)}, bf16[128,512]{1,0:T(8,128)(2,1)S(1)}, u32[]{:S(2)}, u32[]{:S(2)}) collective-permute-start(bf16[128,512]{1,0:T(8,128)(2,1)S(1)} %shard_map.75.d0), channel_id=1, source_target_pairs={{0,12},{1,13},{2,14},{3,15},{4,8},{5,9},{6,10},{7,11},{8,4},{9,5},... | collective-permute-start | bytes 393224 | tf_op jit(solution)/shard_map/ppermute | solution.py:329
  41.5 6.1 %collective-permute-start.1 = (bf16[128,512]{1,0:T(8,128)(2,1)S(1)}, bf16[128,512]{1,0:T(8,128)(2,1)S(1)}, u32[]{:S(2)}, u32[]{:S(2)}) collective-permute-start(bf16[128,512]{1,0:T(8,128)(2,1)S(1)} %shard_map.75.d0), channel_id=1, source_target_pairs={{0,8},{1,9},{2,10},{3,11},{4,12},{5,13},{6,14},{7,15},{8,0},{9,1},... | collective-permute-start | bytes 393224 | tf_op jit(solution)/shard_map/ppermute | solution.py:329
  47.5 2.9 %collective-permute-start = (bf16[128,512]{1,0:T(8,128)(2,1)S(1)}, bf16[128,512]{1,0:T(8,128)(2,1)S(1)}, u32[]{:S(2)}, u32[]{:S(2)}) collective-permute-start(bf16[128,512]{1,0:T(8,128)(2,1)S(1)} %shard_map.75.d0), channel_id=1, source_target_pairs={{0,4},{1,5},{2,6},{3,7},{4,0},{5,1},{6,2},{7,3},{8,12},{9,13},{10,... | collective-permute-start | bytes 393224 | tf_op jit(solution)/shard_map/ppermute | solution.py:329
  50.4 0.0 copy-done
  50.4 0.0 copy-done.1
  50.4 0.0 copy-done.2
  50.4 0.8 shard_map.74
  51.2 10.6 %collective-permute-done.2.d3 = bf16[128,512]{1,0:T(8,128)(2,1)S(1)} collective-permute-done((bf16[128,512]{1,0:T(8,128)(2,1)S(1)}, bf16[128,512]{1,0:T(8,128)(2,1)S(1)}, u32[]{:S(2)}, u32[]{:S(2)}) %collective-permute-start.2) | collective-permute-done | bytes 131104 | tf_op jit(solution)/shard_map/ppermute | solution.py:329
  61.8 9.5 %collective-permute-done.1.d2 = bf16[128,512]{1,0:T(8,128)(2,1)S(1)} collective-permute-done((bf16[128,512]{1,0:T(8,128)(2,1)S(1)}, bf16[128,512]{1,0:T(8,128)(2,1)S(1)}, u32[]{:S(2)}, u32[]{:S(2)}) %collective-permute-start.1) | collective-permute-done | bytes 131104 | tf_op jit(solution)/shard_map/ppermute | solution.py:329
  71.3 0.0 collective-permute-done.d1
  71.3 1.4 %shard_map.76 = bf16[128,8,128]{2,1,0:T(8,128)(2,1)} custom-call(s32[1]{0:T(128)} %bitcast.1.quad_ref, bf16[128,512]{1,0:T(8,128)(2,1)S(1)} %get-tuple-element.12.left_all, bf16[128,512]{1,0:T(8,128)(2,1)S(1)} %get-tuple-element.13.right_all, bf16[128,512]{1,0:T(8,128)(2,1)S(1)} %shard_map.75.d0, bf16[128,512]{1,0:T(8,128)(2,1)S(1)} %collective-permute-done.d1, ...), custom_call_target="tpu_custom_call" | custom-call | flops 100000000 | bytes 1000000 | tf_op jit(solution)/shard_map/pallas_call | solution.py:268
  72.7 0.0 copy-start.3
  72.7 0.0 copy-start.4
  72.7 8.8 %all-to-all-start.1 = ((bf16[128,8,128]{2,1,0:T(8,128)(2,1)}), bf16[128,8,128]{2,1,0:T(8,128)(2,1)S(1)}, u32[]{:S(2)}, u32[]{:S(2)}) async-start(bf16[128,8,128]{2,1,0:T(8,128)(2,1)} %shard_map.76), calls=%async_computation.1 | async-start | bytes 524288 | tf_op jit(solution)/shard_map/all_to_all | solution.py:361
  81.6 0.0 copy-start.5
  81.6 0.0 copy-start.6
  81.6 3.7 %collective-permute-start.3 = (bf16[3,16,2048]{2,1,0:T(8,128)(2,1)S(1)}, bf16[3,16,2048]{2,1,0:T(8,128)(2,1)S(1)}, u32[]{:S(2)}, u32[]{:S(2)}) collective-permute-start(bf16[3,16,2048]{2,1,0:T(8,128)(2,1)S(1)} %get-tuple-element.14), channel_id=1, source_target_pairs={{0,256},{256,0},{1,257},{257,1},{2,258},{258,2},{3,259},{259,3},{4... | collective-permute-start | bytes 589832 | tf_op jit(solution)/shard_map/ppermute | solution.py:326
  85.3 6.1 %collective-permute-done.3.other = bf16[3,16,2048]{2,1,0:T(8,128)(2,1)S(1)} collective-permute-done((bf16[3,16,2048]{2,1,0:T(8,128)(2,1)S(1)}, bf16[3,16,2048]{2,1,0:T(8,128)(2,1)S(1)}, u32[]{:S(2)}, u32[]{:S(2)}) %collective-permute-start.3) | collective-permute-done | bytes 196640 | tf_op jit(solution)/shard_map/ppermute | solution.py:326
  91.4 0.0 copy-done.3
  91.4 0.0 copy-done.4
  91.4 0.0 copy-done.5
  91.4 0.0 copy-done.6
  91.4 1.2 %shard_map.77 = (f32[4,64,1024]{2,1,0:T(8,128)S(1)}, f32[64,1024]{1,0:T(8,128)S(1)}, f32[64,1024]{1,0:T(8,128)S(1)}, f32[1,1024]{1,0:T(1,128)S(1)}) custom-call(s32[1]{0:T(128)} %bitcast.mine_ref, bf16[1,32,2048]{2,1,0:T(8,128)(2,1)S(1)} %copy-done, bf16[1,32,2048]{2,1,0:T(8,128)(2,1)S(1)} %copy-done.1, bf16[1,32,2048]{2,1,0:T(8,128)(2,1)S(1)} %copy-done.2, ...), custom_call_target="tpu_custom_call" | custom-call | flops 100000000 | bytes 1000000 | tf_op jit(solution)/shard_map/pallas_call | solution.py:268
  92.7 1.9 %all-to-all-done.1.home = bf16[128,8,128]{2,1,0:T(8,128)(2,1)S(1)} async-done(((bf16[128,8,128]{2,1,0:T(8,128)(2,1)}), bf16[128,8,128]{2,1,0:T(8,128)(2,1)S(1)}, u32[]{:S(2)}, u32[]{:S(2)}) %all-to-all-start.1) | async-done | bytes 262176 | tf_op jit(solution)/shard_map/all_to_all | solution.py:361
  94.6 1.3 %shard_map.78 = f32[16,2048]{1,0:T(8,128)} custom-call(s32[1]{0:T(128)} %bitcast.mine_ref, bf16[128,8,128]{2,1,0:T(8,128)(2,1)S(1)} %all-to-all-done.1.home, f32[4,64,1024]{2,1,0:T(8,128)S(1)} %get-tuple-element.15.factors, f32[64,1024]{1,0:T(8,128)S(1)} %get-tuple-element.16.rest, f32[64,1024]{1,0:T(8,128)S(1)} %get-tuple-element.17.units, ...), custom_call_target="tpu_custom_call" | custom-call | flops 100000000 | bytes 1000000 | tf_op jit(solution)/shard_map/pallas_call | solution.py:268
Async XLA Ops:
  31.5 18.9 %copy-start = (bf16[1,32,2048]{2,1,0:T(8,128)(2,1)S(1)}, bf16[1,32,2048]{2,1,0:T(8,128)(2,1)}, u32[]{:S(2)}) copy-start(bf16[1,32,2048]{2,1,0:T(8,128)(2,1)} %pair.3) | copy-start | bytes 393220
  31.5 18.9 %copy-start.1 = (bf16[1,32,2048]{2,1,0:T(8,128)(2,1)S(1)}, bf16[1,32,2048]{2,1,0:T(8,128)(2,1)}, u32[]{:S(2)}) copy-start(bf16[1,32,2048]{2,1,0:T(8,128)(2,1)} %saved.3) | copy-start | bytes 393220
  31.5 18.9 %copy-start.2 = (bf16[1,32,2048]{2,1,0:T(8,128)(2,1)S(1)}, bf16[1,32,2048]{2,1,0:T(8,128)(2,1)}, u32[]{:S(2)}) copy-start(bf16[1,32,2048]{2,1,0:T(8,128)(2,1)} %upstream.3) | copy-start | bytes 393220
  31.7 30.1 %collective-permute-start.2 = (bf16[128,512]{1,0:T(8,128)(2,1)S(1)}, bf16[128,512]{1,0:T(8,128)(2,1)S(1)}, u32[]{:S(2)}, u32[]{:S(2)}) collective-permute-start(bf16[128,512]{1,0:T(8,128)(2,1)S(1)} %shard_map.75.d0), channel_id=1, source_target_pairs={{0,12},{1,13},{2,14},{3,15},{4,8},{5,9},{6,10},{7,11},{8,4},{9,5},... | collective-permute-start | bytes 393224 | tf_op jit(solution)/shard_map/ppermute | solution.py:329
  41.5 29.8 %collective-permute-start.1 = (bf16[128,512]{1,0:T(8,128)(2,1)S(1)}, bf16[128,512]{1,0:T(8,128)(2,1)S(1)}, u32[]{:S(2)}, u32[]{:S(2)}) collective-permute-start(bf16[128,512]{1,0:T(8,128)(2,1)S(1)} %shard_map.75.d0), channel_id=1, source_target_pairs={{0,8},{1,9},{2,10},{3,11},{4,12},{5,13},{6,14},{7,15},{8,0},{9,1},... | collective-permute-start | bytes 393224 | tf_op jit(solution)/shard_map/ppermute | solution.py:329
  47.5 23.7 %collective-permute-start = (bf16[128,512]{1,0:T(8,128)(2,1)S(1)}, bf16[128,512]{1,0:T(8,128)(2,1)S(1)}, u32[]{:S(2)}, u32[]{:S(2)}) collective-permute-start(bf16[128,512]{1,0:T(8,128)(2,1)S(1)} %shard_map.75.d0), channel_id=1, source_target_pairs={{0,4},{1,5},{2,6},{3,7},{4,0},{5,1},{6,2},{7,3},{8,12},{9,13},{10,... | collective-permute-start | bytes 393224 | tf_op jit(solution)/shard_map/ppermute | solution.py:329
  72.7 18.7 %copy-start.3 = (bf16[64,320]{1,0:T(8,128)(2,1)S(1)}, bf16[64,320]{1,0:T(8,128)(2,1)}, u32[]{:S(2)}) copy-start(bf16[64,320]{1,0:T(8,128)(2,1)} %w_in.3) | copy-start | bytes 122884
  72.7 18.7 %copy-start.4 = (bf16[64,64]{1,0:T(8,128)(2,1)S(1)}, bf16[64,64]{1,0:T(8,128)(2,1)}, u32[]{:S(2)}) copy-start(bf16[64,64]{1,0:T(8,128)(2,1)} %w_out.1) | copy-start | bytes 24580
  72.7 21.9 %all-to-all-start.1 = ((bf16[128,8,128]{2,1,0:T(8,128)(2,1)}), bf16[128,8,128]{2,1,0:T(8,128)(2,1)S(1)}, u32[]{:S(2)}, u32[]{:S(2)}) async-start(bf16[128,8,128]{2,1,0:T(8,128)(2,1)} %shard_map.76), calls=%async_computation.1 | async-start | bytes 524288 | tf_op jit(solution)/shard_map/all_to_all | solution.py:361
  81.6 9.8 %copy-start.5 = (f32[64]{0:T(128)S(1)}, f32[64]{0:T(128)}, u32[]{:S(2)}) copy-start(f32[64]{0:T(128)} %param.10) | copy-start | bytes 772
  81.6 9.8 %copy-start.6 = (f32[64]{0:T(128)S(1)}, f32[64]{0:T(128)}, u32[]{:S(2)}) copy-start(f32[64]{0:T(128)} %param.11) | copy-start | bytes 772
  81.6 9.8 %collective-permute-start.3 = (bf16[3,16,2048]{2,1,0:T(8,128)(2,1)S(1)}, bf16[3,16,2048]{2,1,0:T(8,128)(2,1)S(1)}, u32[]{:S(2)}, u32[]{:S(2)}) collective-permute-start(bf16[3,16,2048]{2,1,0:T(8,128)(2,1)S(1)} %get-tuple-element.14), channel_id=1, source_target_pairs={{0,256},{256,0},{1,257},{257,1},{2,258},{258,2},{3,259},{259,3},{4... | collective-permute-start | bytes 589832 | tf_op jit(solution)/shard_map/ppermute | solution.py:326

commit v7 on v6

--- a/solution.py
+++ b/solution.py
@@ -71,12 +71,11 @@
     ]
     for move in moves:
         move.start()
-    for n in (3, 4, 5, 6, 0, 1, 2):
+    for n in (3, 5, 0):
         moves[n].wait()
     pair, saved, upstream, in_gain, out_gain, w_in, w_out = copies
     channels = w_out.shape[0]
-    gain_in, gain_out = column(in_gain), column(out_gain)
-    weights, weights_out = w_in[...], w_out[...]
+    gain_in, weights = column(in_gain), w_in[...]
 
     def tiles(ref):
         return jnp.concatenate(
@@ -94,6 +93,9 @@
                 held[at : at + 8, :] = value[8 * c : 8 * c + 8, g * LANES : (g + 1) * LANES]
 
     normed = normalize(tiles(pair), gain_in)[0].astype(BF16)
+    for n in (4, 6, 1, 2):
+        moves[n].wait()
+    gain_out, weights_out = column(out_gain), w_out[...]
     _, unit, inv = normalize(tiles(saved), gain_out)
     up = tiles(upstream)
     mixed = []

time: 96.3 us -> 96.3 us (level)
  no operation moved by 1% of the time
where the time goes in v7:
time: 96.3 us; the launch traced here: 95.9 us
  starting transfers between devices  31.2 us (32%)
  blocking collectives  28.9 us (30%)
  waiting for transfers between devices  28.1 us (29%)
  Pallas kernels  7.61 us (8%)
    all_to_all x1, blocking collectives, body(): lax.all_to_all(send, ('row', 'col'), 0, 0, axis_index_groups=groups, tile...  28.9 us
    ppermute x3, waiting for transfers between devices, body(): lax.ppermute(d_own, 'col', [(z, z ^ near * s) for z in range(cols_n)])  20 us
    ppermute x3, starting transfers between devices, body(): lax.ppermute(d_own, 'col', [(z, z ^ near * s) for z in range(cols_n)])  18.7 us
    all_to_all x1, starting transfers between devices, body(): lax.all_to_all(back, ('tmpl', 'row', 'col'), 0, 0, axis_index_groups=grou...  8.84 us
    pallas_call x6, Pallas kernels, call(): pl.pallas_call(kernel, out_shape=outs, in_specs=[SMEM] * scalars + [space...  7.61 us
    ppermute x1, waiting for transfers between devices, body(): other = lax.ppermute(give, 'tmpl', [(0, 1), (1, 0)])  6.1 us
    ppermute x1, starting transfers between devices, body(): other = lax.ppermute(give, 'tmpl', [(0, 1), (1, 0)])  3.7 us
  transfers between devices with their start and end apart: 5, of which 4 were waited for; matrix products, arithmetic and copies ran while one was open for 0% of the time, Pallas kernels for 2%

profile of v7, /device:TPU:1, one launch (start us, length us, event | category | flops | bytes accessed | tf_op | source)
XLA Modules:
  0.0 95.9 jit_solution(11592038340481593542)
XLA Ops:
  0.0 2.7 %shard_map.73 = bf16[64,24,128]{2,1,0:T(8,128)(2,1)} custom-call(bf16[1,32,2048]{2,1,0:T(8,128)(2,1)} %pair.3, bf16[1,32,2048]{2,1,0:T(8,128)(2,1)} %saved.3, bf16[1,32,2048]{2,1,0:T(8,128)(2,1)} %upstream.3, f32[1,64]{1,0:T(1,128)} %bitcast.4, f32[1,64]{1,0:T(1,128)} %bitcast.7, bf16[64,320]{1,0:T(8,128)(2,1)} %w_in.3, bf16[64,64]{1,0:T(8,128)(2,1)} %w_out.1), custom_call_target="tpu_custom_call" | custom-call | flops 100000000 | bytes 1000000 | tf_op jit(solution)/shard_map/pallas_call | solution.py:270
  2.7 28.9 %all_to_all.10.got = bf16[64,24,128]{2,1,0:T(8,128)(2,1)S(1)} all-to-all(bf16[64,24,128]{2,1,0:T(8,128)(2,1)} %shard_map.73), channel_id=1, replica_groups={{0,1,2,3,16,17,18,19,32,33,34,35,48,49,50,51,64,65,66,67,80,81,82,83,96..., dimensions={0} | all-to-all | bytes 786432 | tf_op jit(solution)/shard_map/all_to_all | solution.py:319
  31.6 0.0 copy-start
  31.6 0.0 copy-start.1
  31.6 0.0 copy-start.2
  31.6 0.2 shard_map.75.d0
  31.8 9.8 %collective-permute-start.2 = (bf16[128,512]{1,0:T(8,128)(2,1)S(1)}, bf16[128,512]{1,0:T(8,128)(2,1)S(1)}, u32[]{:S(2)}, u32[]{:S(2)}) collective-permute-start(bf16[128,512]{1,0:T(8,128)(2,1)S(1)} %shard_map.75.d0), channel_id=1, source_target_pairs={{0,12},{1,13},{2,14},{3,15},{4,8},{5,9},{6,10},{7,11},{8,4},{9,5},... | collective-permute-start | bytes 393224 | tf_op jit(solution)/shard_map/ppermute | solution.py:331
  41.5 6.1 %collective-permute-start.1 = (bf16[128,512]{1,0:T(8,128)(2,1)S(1)}, bf16[128,512]{1,0:T(8,128)(2,1)S(1)}, u32[]{:S(2)}, u32[]{:S(2)}) collective-permute-start(bf16[128,512]{1,0:T(8,128)(2,1)S(1)} %shard_map.75.d0), channel_id=1, source_target_pairs={{0,8},{1,9},{2,10},{3,11},{4,12},{5,13},{6,14},{7,15},{8,0},{9,1},... | collective-permute-start | bytes 393224 | tf_op jit(solution)/shard_map/ppermute | solution.py:331
  47.6 2.9 %collective-permute-start = (bf16[128,512]{1,0:T(8,128)(2,1)S(1)}, bf16[128,512]{1,0:T(8,128)(2,1)S(1)}, u32[]{:S(2)}, u32[]{:S(2)}) collective-permute-start(bf16[128,512]{1,0:T(8,128)(2,1)S(1)} %shard_map.75.d0), channel_id=1, source_target_pairs={{0,4},{1,5},{2,6},{3,7},{4,0},{5,1},{6,2},{7,3},{8,12},{9,13},{10,... | collective-permute-start | bytes 393224 | tf_op jit(solution)/shard_map/ppermute | solution.py:331
  50.5 0.0 copy-done
  50.5 0.0 copy-done.1
  50.5 0.0 copy-done.2
  50.5 0.8 shard_map.74
  51.3 10.6 %collective-permute-done.2.d3 = bf16[128,512]{1,0:T(8,128)(2,1)S(1)} collective-permute-done((bf16[128,512]{1,0:T(8,128)(2,1)S(1)}, bf16[128,512]{1,0:T(8,128)(2,1)S(1)}, u32[]{:S(2)}, u32[]{:S(2)}) %collective-permute-start.2) | collective-permute-done | bytes 131104 | tf_op jit(solution)/shard_map/ppermute | solution.py:331
  61.9 9.5 %collective-permute-done.1.d2 = bf16[128,512]{1,0:T(8,128)(2,1)S(1)} collective-permute-done((bf16[128,512]{1,0:T(8,128)(2,1)S(1)}, bf16[128,512]{1,0:T(8,128)(2,1)S(1)}, u32[]{:S(2)}, u32[]{:S(2)}) %collective-permute-start.1) | collective-permute-done | bytes 131104 | tf_op jit(solution)/shard_map/ppermute | solution.py:331
  71.3 0.0 collective-permute-done.d1
  71.3 1.4 %shard_map.76 = bf16[128,8,128]{2,1,0:T(8,128)(2,1)} custom-call(s32[1]{0:T(128)} %bitcast.1.quad_ref, bf16[128,512]{1,0:T(8,128)(2,1)S(1)} %get-tuple-element.12.left_all, bf16[128,512]{1,0:T(8,128)(2,1)S(1)} %get-tuple-element.13.right_all, bf16[128,512]{1,0:T(8,128)(2,1)S(1)} %shard_map.75.d0, bf16[128,512]{1,0:T(8,128)(2,1)S(1)} %collective-permute-done.d1, ...), custom_call_target="tpu_custom_call" | custom-call | flops 100000000 | bytes 1000000 | tf_op jit(solution)/shard_map/pallas_call | solution.py:270
  72.8 0.0 copy-start.3
  72.8 0.0 copy-start.4
  72.8 8.8 %all-to-all-start.1 = ((bf16[128,8,128]{2,1,0:T(8,128)(2,1)}), bf16[128,8,128]{2,1,0:T(8,128)(2,1)S(1)}, u32[]{:S(2)}, u32[]{:S(2)}) async-start(bf16[128,8,128]{2,1,0:T(8,128)(2,1)} %shard_map.76), calls=%async_computation.1 | async-start | bytes 524288 | tf_op jit(solution)/shard_map/all_to_all | solution.py:363
  81.6 0.0 copy-start.5
  81.6 0.0 copy-start.6
  81.7 3.7 %collective-permute-start.3 = (bf16[3,16,2048]{2,1,0:T(8,128)(2,1)S(1)}, bf16[3,16,2048]{2,1,0:T(8,128)(2,1)S(1)}, u32[]{:S(2)}, u32[]{:S(2)}) collective-permute-start(bf16[3,16,2048]{2,1,0:T(8,128)(2,1)S(1)} %get-tuple-element.14), channel_id=1, source_target_pairs={{0,256},{256,0},{1,257},{257,1},{2,258},{258,2},{3,259},{259,3},{4... | collective-permute-start | bytes 589832 | tf_op jit(solution)/shard_map/ppermute | solution.py:328
  85.4 6.1 %collective-permute-done.3.other = bf16[3,16,2048]{2,1,0:T(8,128)(2,1)S(1)} collective-permute-done((bf16[3,16,2048]{2,1,0:T(8,128)(2,1)S(1)}, bf16[3,16,2048]{2,1,0:T(8,128)(2,1)S(1)}, u32[]{:S(2)}, u32[]{:S(2)}) %collective-permute-start.3) | collective-permute-done | bytes 196640 | tf_op jit(solution)/shard_map/ppermute | solution.py:328
  91.5 0.0 copy-done.3
  91.5 0.0 copy-done.4
  91.5 0.0 copy-done.5
  91.5 0.0 copy-done.6
  91.5 1.2 %shard_map.77 = (f32[4,64,1024]{2,1,0:T(8,128)S(1)}, f32[64,1024]{1,0:T(8,128)S(1)}, f32[64,1024]{1,0:T(8,128)S(1)}, f32[1,1024]{1,0:T(1,128)S(1)}) custom-call(s32[1]{0:T(128)} %bitcast.mine_ref, bf16[1,32,2048]{2,1,0:T(8,128)(2,1)S(1)} %copy-done, bf16[1,32,2048]{2,1,0:T(8,128)(2,1)S(1)} %copy-done.1, bf16[1,32,2048]{2,1,0:T(8,128)(2,1)S(1)} %copy-done.2, ...), custom_call_target="tpu_custom_call" | custom-call | flops 100000000 | bytes 1000000 | tf_op jit(solution)/shard_map/pallas_call | solution.py:270
  92.7 1.9 %all-to-all-done.1.home = bf16[128,8,128]{2,1,0:T(8,128)(2,1)S(1)} async-done(((bf16[128,8,128]{2,1,0:T(8,128)(2,1)}), bf16[128,8,128]{2,1,0:T(8,128)(2,1)S(1)}, u32[]{:S(2)}, u32[]{:S(2)}) %all-to-all-start.1) | async-done | bytes 262176 | tf_op jit(solution)/shard_map/all_to_all | solution.py:363
  94.7 1.3 %shard_map.78 = f32[16,2048]{1,0:T(8,128)} custom-call(s32[1]{0:T(128)} %bitcast.mine_ref, bf16[128,8,128]{2,1,0:T(8,128)(2,1)S(1)} %all-to-all-done.1.home, f32[4,64,1024]{2,1,0:T(8,128)S(1)} %get-tuple-element.15.factors, f32[64,1024]{1,0:T(8,128)S(1)} %get-tuple-element.16.rest, f32[64,1024]{1,0:T(8,128)S(1)} %get-tuple-element.17.units, ...), custom_call_target="tpu_custom_call" | custom-call | flops 100000000 | bytes 1000000 | tf_op jit(solution)/shard_map/pallas_call | solution.py:270
Async XLA Ops:
  31.6 18.9 %copy-start = (bf16[1,32,2048]{2,1,0:T(8,128)(2,1)S(1)}, bf16[1,32,2048]{2,1,0:T(8,128)(2,1)}, u32[]{:S(2)}) copy-start(bf16[1,32,2048]{2,1,0:T(8,128)(2,1)} %pair.3) | copy-start | bytes 393220
  31.6 18.9 %copy-start.1 = (bf16[1,32,2048]{2,1,0:T(8,128)(2,1)S(1)}, bf16[1,32,2048]{2,1,0:T(8,128)(2,1)}, u32[]{:S(2)}) copy-start(bf16[1,32,2048]{2,1,0:T(8,128)(2,1)} %saved.3) | copy-start | bytes 393220
  31.6 18.9 %copy-start.2 = (bf16[1,32,2048]{2,1,0:T(8,128)(2,1)S(1)}, bf16[1,32,2048]{2,1,0:T(8,128)(2,1)}, u32[]{:S(2)}) copy-start(bf16[1,32,2048]{2,1,0:T(8,128)(2,1)} %upstream.3) | copy-start | bytes 393220
  31.8 30.1 %collective-permute-start.2 = (bf16[128,512]{1,0:T(8,128)(2,1)S(1)}, bf16[128,512]{1,0:T(8,128)(2,1)S(1)}, u32[]{:S(2)}, u32[]{:S(2)}) collective-permute-start(bf16[128,512]{1,0:T(8,128)(2,1)S(1)} %shard_map.75.d0), channel_id=1, source_target_pairs={{0,12},{1,13},{2,14},{3,15},{4,8},{5,9},{6,10},{7,11},{8,4},{9,5},... | collective-permute-start | bytes 393224 | tf_op jit(solution)/shard_map/ppermute | solution.py:331
  41.5 29.8 %collective-permute-start.1 = (bf16[128,512]{1,0:T(8,128)(2,1)S(1)}, bf16[128,512]{1,0:T(8,128)(2,1)S(1)}, u32[]{:S(2)}, u32[]{:S(2)}) collective-permute-start(bf16[128,512]{1,0:T(8,128)(2,1)S(1)} %shard_map.75.d0), channel_id=1, source_target_pairs={{0,8},{1,9},{2,10},{3,11},{4,12},{5,13},{6,14},{7,15},{8,0},{9,1},... | collective-permute-start | bytes 393224 | tf_op jit(solution)/shard_map/ppermute | solution.py:331
  47.6 23.7 %collective-permute-start = (bf16[128,512]{1,0:T(8,128)(2,1)S(1)}, bf16[128,512]{1,0:T(8,128)(2,1)S(1)}, u32[]{:S(2)}, u32[]{:S(2)}) collective-permute-start(bf16[128,512]{1,0:T(8,128)(2,1)S(1)} %shard_map.75.d0), channel_id=1, source_target_pairs={{0,4},{1,5},{2,6},{3,7},{4,0},{5,1},{6,2},{7,3},{8,12},{9,13},{10,... | collective-permute-start | bytes 393224 | tf_op jit(solution)/shard_map/ppermute | solution.py:331
  72.8 18.7 %copy-start.3 = (bf16[64,320]{1,0:T(8,128)(2,1)S(1)}, bf16[64,320]{1,0:T(8,128)(2,1)}, u32[]{:S(2)}) copy-start(bf16[64,320]{1,0:T(8,128)(2,1)} %w_in.3) | copy-start | bytes 122884
  72.8 18.7 %copy-start.4 = (bf16[64,64]{1,0:T(8,128)(2,1)S(1)}, bf16[64,64]{1,0:T(8,128)(2,1)}, u32[]{:S(2)}) copy-start(bf16[64,64]{1,0:T(8,128)(2,1)} %w_out.1) | copy-start | bytes 24580
  72.8 21.9 %all-to-all-start.1 = ((bf16[128,8,128]{2,1,0:T(8,128)(2,1)}), bf16[128,8,128]{2,1,0:T(8,128)(2,1)S(1)}, u32[]{:S(2)}, u32[]{:S(2)}) async-start(bf16[128,8,128]{2,1,0:T(8,128)(2,1)} %shard_map.76), calls=%async_computation.1 | async-start | bytes 524288 | tf_op jit(solution)/shard_map/all_to_all | solution.py:363
  81.6 9.8 %copy-start.5 = (f32[64]{0:T(128)S(1)}, f32[64]{0:T(128)}, u32[]{:S(2)}) copy-start(f32[64]{0:T(128)} %param.10) | copy-start | bytes 772
  81.6 9.8 %copy-start.6 = (f32[64]{0:T(128)S(1)}, f32[64]{0:T(128)}, u32[]{:S(2)}) copy-start(f32[64]{0:T(128)} %param.11) | copy-start | bytes 772
  81.7 9.8 %collective-permute-start.3 = (bf16[3,16,2048]{2,1,0:T(8,128)(2,1)S(1)}, bf16[3,16,2048]{2,1,0:T(8,128)(2,1)S(1)}, u32[]{:S(2)}, u32[]{:S(2)}) collective-permute-start(bf16[3,16,2048]{2,1,0:T(8,128)(2,1)S(1)} %get-tuple-element.14), channel_id=1, source_target_pairs={{0,256},{256,0},{1,257},{257,1},{2,258},{258,2},{3,259},{259,3},{4... | collective-permute-start | bytes 589832 | tf_op jit(solution)/shard_map/ppermute | solution.py:328
